TPU v7x, 512 devices: a whole 4x8x8 slice. The times are simulated.
512 devices in a mesh: gx: 32 (over y, x), gy: 16 (over z, core).
Axes of the slice: x: 4, y: 8, z: 8, core: 2. Of those that a mesh axis runs over, the one named last changes fastest.
Arguments:
- source: float32 [256, 256, 512], P('gx', 'gy'), may hold values from -6 to 6
- face_coef: bfloat16 [3, 256, 256, 512], P(None, 'gx', 'gy'), may hold values from 0.25 to 4
Outputs:
- potential: float32 [256, 256, 512], P('gx', 'gy')
All inputs are finite; a program needn't handle non-finite values.
Results may differ from a plain program's by a relative error of at most 0.0003.
Values sent between devices are 32-bit elements; how exact they have to be, the bound alone decides.
A program may use at most 64 MiB of HBM per device.

v0:
```python
import math

import jax
import jax.numpy as jnp
from jax import lax
from jax.sharding import PartitionSpec as P

LEVELS = 3
SWEEPS = 2


MASS = 0.002


def with_halo(block, sides, width):
    for axis, dim in sides:
        count = lax.axis_size(axis)
        forward = [(i, i + 1) for i in range(count - 1)]
        forward.append((count - 1, 0))
        backward = [(target, source) for source, target in forward]
        low = lax.ppermute(
            lax.slice_in_dim(block, block.shape[dim] - width, None, axis=dim), axis, forward
        )
        high = lax.ppermute(lax.slice_in_dim(block, 0, width, axis=dim), axis, backward)
        block = jnp.concatenate([low, block, high], axis=dim)
    return block


def shifted(block, axis, distance):
    devices = range(lax.axis_size(axis))
    route = [((i - distance) % len(devices), i) for i in devices]
    return lax.ppermute(block, axis, route)


def coarsen(couplings):
    east_face = couplings[0][1::2]
    east_face = (
        east_face[:, 0::2, 0::2]
        + east_face[:, 1::2, 0::2]
        + east_face[:, 0::2, 1::2]
        + east_face[:, 1::2, 1::2]
    )
    north_face = couplings[1][:, 1::2]
    north_face = (
        north_face[0::2, :, 0::2]
        + north_face[1::2, :, 0::2]
        + north_face[0::2, :, 1::2]
        + north_face[1::2, :, 1::2]
    )
    upper_face = couplings[2][:, :, 1::2]
    upper_face = (
        upper_face[0::2, 0::2]
        + upper_face[1::2, 0::2]
        + upper_face[0::2, 1::2]
        + upper_face[1::2, 1::2]
    )
    return jnp.stack((east_face, north_face, upper_face)) * 0.0625


def restrict(residual):
    dims = residual.shape
    return residual.reshape(dims[0] // 2, 2, dims[1] // 2, 2, dims[2] // 2, 2).mean(axis=(1, 3, 5))


def prolong(correction):
    return jnp.repeat(jnp.repeat(jnp.repeat(correction, 2, 0), 2, 1), 2, 2)


def pad_single(potential):
    return with_halo(potential, (("gx", 0), ("gy", 1)), 1)


def lower_tables(couplings):
    previous_rows = shifted(couplings[0][-1:], "gx", 1)
    previous_cols = shifted(couplings[1][:, -1:], "gy", 1)
    east_back = jnp.concatenate((previous_rows, couplings[0][:-1]), axis=0)
    north_back = jnp.concatenate((previous_cols, couplings[1][:, :-1]), axis=1)
    upper_back = jnp.roll(couplings[2], 1, 2)
    diagonal = (
        MASS + couplings[0] + east_back + couplings[1] + north_back + couplings[2] + upper_back
    )
    return (
        (couplings[0], couplings[1], couplings[2]),
        (east_back, north_back, upper_back),
        diagonal,
    )


def region_parity(local_dims, extent):
    row_ids = (
        lax.axis_index("gx") * local_dims[0]
        - extent
        + jnp.arange(local_dims[0] + 2 * extent, dtype=jnp.int32)
    )
    col_ids = (
        lax.axis_index("gy") * local_dims[1]
        - extent
        + jnp.arange(local_dims[1] + 2 * extent, dtype=jnp.int32)
    )
    depth_ids = jnp.arange(local_dims[2], dtype=jnp.int32)
    return (row_ids[:, None, None] + col_ids[None, :, None] + depth_ids[None, None, :]) % 2


def neighbour_terms(padded, offset, couplings, lagged):
    row_count = couplings[0].shape[0]
    col_count = couplings[0].shape[1]
    centre = padded[offset : offset + row_count, offset : offset + col_count]
    summed = (
        couplings[0] * padded[offset + 1 : offset + 1 + row_count, offset : offset + col_count]
        + lagged[0] * padded[offset - 1 : offset - 1 + row_count, offset : offset + col_count]
    )
    summed = (
        summed
        + couplings[1] * padded[offset : offset + row_count, offset + 1 : offset + 1 + col_count]
        + lagged[1] * padded[offset : offset + row_count, offset - 1 : offset - 1 + col_count]
    )
    summed = summed + couplings[2] * jnp.roll(centre, -1, 2) + lagged[2] * jnp.roll(centre, 1, 2)
    return (centre, summed)


def relax_colour(padded, offset, tables, right_side, parity, colour):
    centre, summed = neighbour_terms(padded, offset, tables[0], tables[1])
    return jnp.where(parity == colour, (right_side + summed) / tables[2], centre)


def hartley_table(row_ids, col_ids, length):
    angles = (row_ids[:, None] * col_ids[None, :] % length).astype(jnp.float32) * (
        2.0 * math.pi / length
    )
    return jnp.cos(angles) + jnp.sin(angles)


def eigenvalues(row_ids, col_ids, depth_ids, lengths, averages):
    parts_list = []
    for axis_index, wave_ids in enumerate((row_ids, col_ids, depth_ids)):
        wave = wave_ids.astype(jnp.float32) * (2.0 * math.pi / lengths[axis_index])
        parts_list.append(2.0 * averages[axis_index] * (1.0 - jnp.cos(wave)))
    return (
        MASS
        + parts_list[0][:, None, None]
        + parts_list[1][None, :, None]
        + parts_list[2][None, None, :]
    )


def coarse_solve(right_side, averages):
    local_rows, local_cols, depth_count = right_side.shape
    total_rows = local_rows * lax.axis_size("gx")
    total_cols = local_cols * lax.axis_size("gy")
    row_ids = lax.axis_index("gx") * local_rows + jnp.arange(local_rows, dtype=jnp.int32)
    col_ids = lax.axis_index("gy") * local_cols + jnp.arange(local_cols, dtype=jnp.int32)
    depth_ids = jnp.arange(depth_count, dtype=jnp.int32)
    depth_table = hartley_table(depth_ids, depth_ids, depth_count)
    lengths = (total_rows, total_cols, depth_count)
    normaliser = float(total_rows * total_cols * depth_count)

    def along_depth(values):
        return jnp.einsum("abz,zk->abk", values, depth_table, precision=lax.Precision.HIGHEST)

    def along_rows(values):

        def accumulate(running, incoming, anchor):
            kernel = hartley_table(
                row_ids, jnp.arange(incoming.shape[0], dtype=jnp.int32), total_rows
            )
            return jnp.einsum("ij,jbz->ibz", kernel, incoming, precision=lax.Precision.HIGHEST)

        return accumulate(
            jnp.zeros_like(values), lax.all_gather(values, "gx", axis=0, tiled=True), jnp.int32(0)
        )

    def along_cols(values):

        def accumulate(running, incoming, anchor):
            kernel = hartley_table(
                col_ids, jnp.arange(incoming.shape[1], dtype=jnp.int32), total_cols
            )
            return jnp.einsum("ij,ajz->aiz", kernel, incoming, precision=lax.Precision.HIGHEST)

        return accumulate(
            jnp.zeros_like(values), lax.all_gather(values, "gy", axis=1, tiled=True), jnp.int32(0)
        )

    spectrum = along_cols(along_rows(along_depth(right_side)))
    spectrum = spectrum / (eigenvalues(row_ids, col_ids, depth_ids, lengths, averages) * normaliser)
    return along_depth(along_cols(along_rows(spectrum)))


def multigrid_cycle(right_side, face_list, averages, level_index):
    if level_index == LEVELS - 1:
        return coarse_solve(right_side, averages)
    couplings = face_list[level_index]
    inner_parity = region_parity(right_side.shape, 0)
    inner_tables = lower_tables(couplings)

    def sweep_all(potential):
        for sweep_index in range(SWEEPS):
            for colour in (0, 1):
                potential = relax_colour(
                    pad_single(potential), 1, inner_tables, right_side, inner_parity, colour
                )
        return potential

    potential = sweep_all(jnp.zeros_like(right_side))
    centre, summed = neighbour_terms(pad_single(potential), 1, inner_tables[0], inner_tables[1])
    residual = right_side - (inner_tables[2] * centre - summed)
    correction = multigrid_cycle(restrict(residual), face_list, averages, level_index + 1)
    potential = potential + prolong(correction)
    return sweep_all(potential)


def shards(source, face_coef):
    face_list = [face_coef.astype(jnp.float32)]
    for level_index in range(LEVELS - 1):
        face_list.append(coarsen(face_list[-1]))
    coarsest = face_list[-1]
    cell_count = coarsest[0].size * lax.axis_size("gx") * lax.axis_size("gy")
    averages = lax.psum(jnp.sum(coarsest, axis=(1, 2, 3)), ("gx", "gy")) / cell_count
    return multigrid_cycle(source, face_list, averages, 0)


def solution(mesh):
    return jax.shard_map(
        shards,
        mesh=mesh,
        in_specs=(P("gx", "gy", None), P(None, "gx", "gy", None)),
        out_specs=P("gx", "gy", None),
        check_vma=False,
    )
```

profile of v0, /device:TPU:1, one launch (start us, length us, event | category | flops | bytes accessed | tf_op | source)
XLA Modules:
  0.0 557.1 jit_solution(8979062184947116813)
XLA Ops:
  0.0 8.1 %collective-permute-start = (f32[1,16,512]{2,1,0:T(8,128)S(1)}, f32[1,16,512]{2,1,0:T(8,128)S(1)}, u32[]{:S(2)}, u32[]{:S(2)}) collective-permute-start(f32[1,16,512]{2,1,0:T(8,128)S(1)} %broadcast.237), channel_id=1, source_target_pairs={{16,0},{32,16},{48,32},{64,48},{80,64},{96,80},{112,96},{128,112},... | collective-permute-start | bytes 98312 | tf_op jit(solution)/shard_map/ppermute | solution.py:24
  10.0 6.7 %collective-permute-start.22 = (f32[1,8,256]{2,1,0:T(8,128)S(1)}, f32[1,8,256]{2,1,0:T(8,128)S(1)}, u32[]{:S(2)}, u32[]{:S(2)}) collective-permute-start(f32[1,8,256]{2,1,0:T(8,128)S(1)} %broadcast.239), channel_id=1, source_target_pairs={{16,0},{32,16},{48,32},{64,48},{80,64},{96,80},{112,96},{128,112},... | collective-permute-start | bytes 24584 | tf_op jit(solution)/shard_map/ppermute | solution.py:24
  19.9 3.5 collective-permute-start.4
  29.2 4.5 slice.971
  43.1 101.9 %psum.7 = f32[3]{0:T(128)S(1)} all-reduce(f32[3]{0:T(128)S(1)} %fusion.239), channel_id=1, replica_groups=mesh['gx'=32,'gy'=16] {'gx','gy'}, use_global_device_ids=true, to_apply=%region_3.4 | all-reduce | flops 3 | bytes 24 | tf_op jit(solution)/shard_map/psum | solution.py:218
  158.5 4.9 collective-permute-start.6
  165.6 5.7 %collective-permute-done.7 = f32[1,16,512]{2,1,0:T(8,128)S(1)} collective-permute-done((f32[1,16,512]{2,1,0:T(8,128)S(1)}, f32[1,16,512]{2,1,0:T(8,128)S(1)}, u32[]{:S(2)}, u32[]{:S(2)}) %collective-permute-start.7) | collective-permute-done | bytes 32800 | tf_op jit(solution)/shard_map/ppermute | solution.py:21
  171.4 4.4 collective-permute-start.8
  182.9 4.5 collective-permute-done.11
  187.4 4.4 collective-permute-start.12
  199.0 4.5 collective-permute-done.15
  203.5 4.4 collective-permute-start.16
  215.0 4.5 collective-permute-done.19
  219.5 4.4 collective-permute-start.20
  225.5 18.1 %reshape.184 = f32[4,2,8,2,256,2]{5,4,3,2,1,0:T(8,128)} reshape(f32[8,16,512]{2,1,0:T(8,128)S(1)} %fusion.64) | data formatting | bytes 524288 | tf_op jit(solution)/shard_map/reshape | solution.py:62
  243.7 7.0 %reduce_sum.27 = f32[4,8,256]{2,1,0:T(8,128)S(1)} reduce(f32[4,2,8,2,256,2]{5,4,3,2,1,0:T(8,128)} %reshape.184, f32[]{:T(128)} %constant.115.clone.1), dimensions={1,3,5}, to_apply=%region_0.0 | reduce | flops 57344 | bytes 294916 | tf_op jit(solution)/shard_map/reduce_sum | solution.py:62
  256.2 4.3 collective-permute-done.29
  260.5 4.4 collective-permute-start.30
  271.5 4.3 collective-permute-done.33
  275.8 4.3 collective-permute-start.34
  286.8 4.3 collective-permute-done.37
  291.0 4.3 collective-permute-start.38
  302.0 4.3 collective-permute-done.41
  306.3 4.3 collective-permute-start.42
  311.8 3.4 reshape.185
  317.5 28.5 %all_gather.12 = f32[64,4,128]{2,1,0:T(4,128)S(1)} all-gather(f32[2,4,128]{2,1,0:T(4,128)S(1)} %fusion.121), channel_id=1, replica_groups=mesh['gx'=32,'gy'=16] {'gx'}, dimensions={0}, use_global_device_ids=true | all-gather | bytes 135168 | tf_op jit(solution)/shard_map/all_gather | solution.py:169
  346.3 25.7 %all_gather.13 = f32[2,64,128]{2,0,1:T(2,128)S(1)} all-gather(f32[2,4,128]{2,0,1:T(2,128)S(1)} %fusion.114), channel_id=1, replica_groups=mesh['gx'=32,'gy'=16] {'gy'}, dimensions={1}, use_global_device_ids=true | all-gather | bytes 69632 | tf_op jit(solution)/shard_map/all_gather | solution.py:181
  372.2 29.0 %all_gather.14 = f32[64,4,128]{2,1,0:T(4,128)S(1)} all-gather(f32[2,4,128]{2,1,0:T(4,128)S(1)} %fusion), channel_id=1, replica_groups=mesh['gx'=32,'gy'=16] {'gx'}, dimensions={0}, use_global_device_ids=true | all-gather | bytes 135168 | tf_op jit(solution)/shard_map/all_gather | solution.py:169
  401.5 24.6 %all_gather.15 = f32[2,64,128]{2,0,1:T(2,128)S(1)} all-gather(f32[2,4,128]{2,0,1:T(2,128)S(1)} %fusion.112), channel_id=1, replica_groups=mesh['gx'=32,'gy'=16] {'gy'}, dimensions={1}, use_global_device_ids=true | all-gather | bytes 69632 | tf_op jit(solution)/shard_map/all_gather | solution.py:181
  427.3 4.3 collective-permute-start.44
  433.6 5.7 %collective-permute-done.45 = f32[1,8,256]{2,1,0:T(8,128)S(1)} collective-permute-done((f32[1,8,256]{2,1,0:T(8,128)S(1)}, f32[1,8,256]{2,1,0:T(8,128)S(1)}, u32[]{:S(2)}, u32[]{:S(2)}) %collective-permute-start.45) | collective-permute-done | bytes 8224 | tf_op jit(solution)/shard_map/ppermute | solution.py:21
  444.5 3.4 collective-permute-start.49
  447.9 4.3 collective-permute-done.49
  452.2 4.0 collective-permute-start.50
  462.9 4.3 collective-permute-done.53
  467.1 4.3 collective-permute-start.54
  474.6 3.6 collective-permute-start.57
  478.3 4.3 collective-permute-done.57
  482.6 4.3 collective-permute-start.58
  497.8 4.5 collective-permute-done.61
  502.3 4.3 collective-permute-start.62
  513.7 4.5 collective-permute-done.65
  518.2 4.4 collective-permute-start.66
  529.8 4.5 collective-permute-done.69
  534.3 4.4 collective-permute-start.70
  542.3 3.4 collective-permute-start.73
  545.8 4.5 collective-permute-done.73
  550.3 4.4 collective-permute-start.74
  (291 shorter events, 136.0 us)
Async XLA Ops:
  0.0 148.2 %collective-permute-start = (f32[1,16,512]{2,1,0:T(8,128)S(1)}, f32[1,16,512]{2,1,0:T(8,128)S(1)}, u32[]{:S(2)}, u32[]{:S(2)}) collective-permute-start(f32[1,16,512]{2,1,0:T(8,128)S(1)} %broadcast.237), channel_id=1, source_target_pairs={{16,0},{32,16},{48,32},{64,48},{80,64},{96,80},{112,96},{128,112},... | collective-permute-start | bytes 98312 | tf_op jit(solution)/shard_map/ppermute | solution.py:24
  8.1 142.1 %collective-permute-start.2 = (f32[1,16,512]{2,1,0:T(8,128)S(1)}, f32[1,16,512]{2,1,0:T(8,128)S(1)}, u32[]{:S(2)}, u32[]{:S(2)}) collective-permute-start(f32[1,16,512]{2,1,0:T(8,128)S(1)} %broadcast.237), channel_id=1, source_target_pairs={{0,16},{16,32},{32,48},{48,64},{64,80},{80,96},{96,112},{112,128},... | collective-permute-start | bytes 98312 | tf_op jit(solution)/shard_map/ppermute | solution.py:21
  10.0 142.1 %collective-permute-start.22 = (f32[1,8,256]{2,1,0:T(8,128)S(1)}, f32[1,8,256]{2,1,0:T(8,128)S(1)}, u32[]{:S(2)}, u32[]{:S(2)}) collective-permute-start(f32[1,8,256]{2,1,0:T(8,128)S(1)} %broadcast.239), channel_id=1, source_target_pairs={{16,0},{32,16},{48,32},{64,48},{80,64},{96,80},{112,96},{128,112},... | collective-permute-start | bytes 24584 | tf_op jit(solution)/shard_map/ppermute | solution.py:24
  16.7 135.4 %collective-permute-start.24 = (f32[1,8,256]{2,1,0:T(8,128)S(1)}, f32[1,8,256]{2,1,0:T(8,128)S(1)}, u32[]{:S(2)}, u32[]{:S(2)}) collective-permute-start(f32[1,8,256]{2,1,0:T(8,128)S(1)} %broadcast.239), channel_id=1, source_target_pairs={{0,16},{16,32},{32,48},{48,64},{64,80},{80,96},{96,112},{112,128},... | collective-permute-start | bytes 24584 | tf_op jit(solution)/shard_map/ppermute | solution.py:21
  19.9 134.0 %collective-permute-start.4 = (f32[8,1,512]{2,0,1:T(8,128)S(1)}, f32[8,1,512]{2,0,1:T(8,128)S(1)}, u32[]{:S(2)}, u32[]{:S(2)}) collective-permute-start(f32[8,1,512]{2,0,1:T(8,128)S(1)} %copy.457), channel_id=1, source_target_pairs={{15,0},{0,1},{1,2},{2,3},{3,4},{4,5},{5,6},{6,7},{7,8},{8,9},{9,10... | collective-permute-start | bytes 49160 | tf_op jit(solution)/shard_map/ppermute | solution.py:32
  148.2 8.1 %collective-permute-start.1 = (f32[1,16,512]{2,1,0:T(8,128)S(1)}, f32[1,16,512]{2,1,0:T(8,128)S(1)}, u32[]{:S(2)}, u32[]{:S(2)}) collective-permute-start(f32[1,16,512]{2,1,0:T(8,128)S(1)} %slice_bitcast_fusion.7), channel_id=1, source_target_pairs={{496,0},{0,16},{16,32},{32,48},{48,64},{64,80},{80,96},{96,112},{1... | collective-permute-start | bytes 98312 | tf_op jit(solution)/shard_map/ppermute | solution.py:32
  150.2 100.5 %collective-permute-start.26 = (f32[4,1,256]{2,1,0:T(1,128)S(1)}, f32[4,1,256]{2,1,0:T(1,128)S(1)}, u32[]{:S(2)}, u32[]{:S(2)}) collective-permute-start(f32[4,1,256]{2,1,0:T(1,128)S(1)} %slice.1193), channel_id=1, source_target_pairs={{15,0},{0,1},{1,2},{2,3},{3,4},{4,5},{5,6},{6,7},{7,8},{8,9},{9,10... | collective-permute-start | bytes 12296 | tf_op jit(solution)/shard_map/ppermute | solution.py:32
  152.1 5.9 %collective-permute-start.3 = (f32[10,1,512]{2,1,0:T(1,128)S(1)}, f32[10,1,512]{2,1,0:T(1,128)S(1)}, u32[]{:S(2)}, u32[]{:S(2)}) collective-permute-start(f32[10,1,512]{2,1,0:T(1,128)S(1)} %get-tuple-element.26), channel_id=1, source_target_pairs={{1,0},{2,1},{3,2},{4,3},{5,4},{6,5},{7,6},{8,7},{9,8},{10,9},{11,1... | collective-permute-start | bytes 61448 | tf_op jit(solution)/shard_map/ppermute | solution.py:24
  152.2 5.9 %collective-permute-start.5 = (f32[10,1,512]{2,1,0:T(1,128)S(1)}, f32[10,1,512]{2,1,0:T(1,128)S(1)}, u32[]{:S(2)}, u32[]{:S(2)}) collective-permute-start(f32[10,1,512]{2,1,0:T(1,128)S(1)} %get-tuple-element.27), channel_id=1, source_target_pairs={{0,1},{1,2},{2,3},{3,4},{4,5},{5,6},{6,7},{7,8},{8,9},{9,10},{10,1... | collective-permute-start | bytes 61448 | tf_op jit(solution)/shard_map/ppermute | solution.py:21
  153.9 96.7 %collective-permute-start.23 = (f32[1,8,256]{2,1,0:T(8,128)S(1)}, f32[1,8,256]{2,1,0:T(8,128)S(1)}, u32[]{:S(2)}, u32[]{:S(2)}) collective-permute-start(f32[1,8,256]{2,1,0:T(8,128)S(1)} %slice_bitcast_fusion.9), channel_id=1, source_target_pairs={{496,0},{0,16},{16,32},{32,48},{48,64},{64,80},{80,96},{96,112},{1... | collective-permute-start | bytes 24584 | tf_op jit(solution)/shard_map/ppermute | solution.py:32
  156.4 94.3 %collective-permute-start.25 = (f32[6,1,256]{2,1,0:T(1,128)S(1)}, f32[6,1,256]{2,1,0:T(1,128)S(1)}, u32[]{:S(2)}, u32[]{:S(2)}) collective-permute-start(f32[6,1,256]{2,1,0:T(1,128)S(1)} %get-tuple-element.95), channel_id=1, source_target_pairs={{1,0},{2,1},{3,2},{4,3},{5,4},{6,5},{7,6},{8,7},{9,8},{10,9},{11,1... | collective-permute-start | bytes 18440 | tf_op jit(solution)/shard_map/ppermute | solution.py:24
  158.5 7.1 %collective-permute-start.6 = (f32[1,16,512]{2,1,0:T(8,128)S(1)}, f32[1,16,512]{2,1,0:T(8,128)S(1)}, u32[]{:S(2)}, u32[]{:S(2)}) collective-permute-start(f32[1,16,512]{2,1,0:T(8,128)S(1)} %get-tuple-element.75), channel_id=1, source_target_pairs={{16,0},{32,16},{48,32},{64,48},{80,64},{96,80},{112,96},{128,112},... | collective-permute-start | bytes 98312 | tf_op jit(solution)/shard_map/ppermute | solution.py:24
  163.4 8.0 %collective-permute-start.7 = (f32[1,16,512]{2,1,0:T(8,128)S(1)}, f32[1,16,512]{2,1,0:T(8,128)S(1)}, u32[]{:S(2)}, u32[]{:S(2)}) collective-permute-start(f32[1,16,512]{2,1,0:T(8,128)S(1)} %get-tuple-element.74), channel_id=1, source_target_pairs={{0,16},{16,32},{32,48},{48,64},{64,80},{80,96},{96,112},{112,128},... | collective-permute-start | bytes 98312 | tf_op jit(solution)/shard_map/ppermute | solution.py:21
  177.5 5.4 collective-permute-start.10
  179.4 8.0 %collective-permute-start.11 = (f32[1,16,512]{2,1,0:T(8,128)S(1)}, f32[1,16,512]{2,1,0:T(8,128)S(1)}, u32[]{:S(2)}, u32[]{:S(2)}) collective-permute-start(f32[1,16,512]{2,1,0:T(8,128)S(1)} %get-tuple-element.68), channel_id=1, source_target_pairs={{0,16},{16,32},{32,48},{48,64},{64,80},{80,96},{96,112},{112,128},... | collective-permute-start | bytes 98312 | tf_op jit(solution)/shard_map/ppermute | solution.py:21
  187.4 5.3 collective-permute-start.12
  193.5 5.4 collective-permute-start.14
  195.5 8.0 %collective-permute-start.15 = (f32[1,16,512]{2,1,0:T(8,128)S(1)}, f32[1,16,512]{2,1,0:T(8,128)S(1)}, u32[]{:S(2)}, u32[]{:S(2)}) collective-permute-start(f32[1,16,512]{2,1,0:T(8,128)S(1)} %get-tuple-element.62), channel_id=1, source_target_pairs={{0,16},{16,32},{32,48},{48,64},{64,80},{80,96},{96,112},{112,128},... | collective-permute-start | bytes 98312 | tf_op jit(solution)/shard_map/ppermute | solution.py:21
  203.5 5.3 collective-permute-start.16
  209.6 5.4 collective-permute-start.18
  211.5 8.0 %collective-permute-start.19 = (f32[1,16,512]{2,1,0:T(8,128)S(1)}, f32[1,16,512]{2,1,0:T(8,128)S(1)}, u32[]{:S(2)}, u32[]{:S(2)}) collective-permute-start(f32[1,16,512]{2,1,0:T(8,128)S(1)} %get-tuple-element.56), channel_id=1, source_target_pairs={{0,16},{16,32},{32,48},{48,64},{64,80},{80,96},{96,112},{112,128},... | collective-permute-start | bytes 98312 | tf_op jit(solution)/shard_map/ppermute | solution.py:21
  224.8 25.9 %collective-permute-start.27 = (f32[6,1,256]{2,1,0:T(1,128)S(1)}, f32[6,1,256]{2,1,0:T(1,128)S(1)}, u32[]{:S(2)}, u32[]{:S(2)}) collective-permute-start(f32[6,1,256]{2,1,0:T(1,128)S(1)} %get-tuple-element.96), channel_id=1, source_target_pairs={{0,1},{1,2},{2,3},{3,4},{4,5},{5,6},{6,7},{7,8},{8,9},{9,10},{10,1... | collective-permute-start | bytes 18440 | tf_op jit(solution)/shard_map/ppermute | solution.py:21
  250.8 5.4 collective-permute-start.28
  252.7 7.7 %collective-permute-start.29 = (f32[1,8,256]{2,1,0:T(8,128)S(1)}, f32[1,8,256]{2,1,0:T(8,128)S(1)}, u32[]{:S(2)}, u32[]{:S(2)}) collective-permute-start(f32[1,8,256]{2,1,0:T(8,128)S(1)} %get-tuple-element.143), channel_id=1, source_target_pairs={{0,16},{16,32},{32,48},{48,64},{64,80},{80,96},{96,112},{112,128},... | collective-permute-start | bytes 24584 | tf_op jit(solution)/shard_map/ppermute | solution.py:21
  266.2 5.4 collective-permute-start.32
  268.1 7.7 %collective-permute-start.33 = (f32[1,8,256]{2,1,0:T(8,128)S(1)}, f32[1,8,256]{2,1,0:T(8,128)S(1)}, u32[]{:S(2)}, u32[]{:S(2)}) collective-permute-start(f32[1,8,256]{2,1,0:T(8,128)S(1)} %get-tuple-element.137), channel_id=1, source_target_pairs={{0,16},{16,32},{32,48},{48,64},{64,80},{80,96},{96,112},{112,128},... | collective-permute-start | bytes 24584 | tf_op jit(solution)/shard_map/ppermute | solution.py:21
  281.4 5.4 collective-permute-start.36
  283.3 7.7 %collective-permute-start.37 = (f32[1,8,256]{2,1,0:T(8,128)S(1)}, f32[1,8,256]{2,1,0:T(8,128)S(1)}, u32[]{:S(2)}, u32[]{:S(2)}) collective-permute-start(f32[1,8,256]{2,1,0:T(8,128)S(1)} %get-tuple-element.131), channel_id=1, source_target_pairs={{0,16},{16,32},{32,48},{48,64},{64,80},{80,96},{96,112},{112,128},... | collective-permute-start | bytes 24584 | tf_op jit(solution)/shard_map/ppermute | solution.py:21
  296.6 5.4 collective-permute-start.40
  298.5 7.7 %collective-permute-start.41 = (f32[1,8,256]{2,1,0:T(8,128)S(1)}, f32[1,8,256]{2,1,0:T(8,128)S(1)}, u32[]{:S(2)}, u32[]{:S(2)}) collective-permute-start(f32[1,8,256]{2,1,0:T(8,128)S(1)} %get-tuple-element.125), channel_id=1, source_target_pairs={{0,16},{16,32},{32,48},{48,64},{64,80},{80,96},{96,112},{112,128},... | collective-permute-start | bytes 24584 | tf_op jit(solution)/shard_map/ppermute | solution.py:21
  427.3 6.3 %collective-permute-start.44 = (f32[1,8,256]{2,1,0:T(8,128)S(1)}, f32[1,8,256]{2,1,0:T(8,128)S(1)}, u32[]{:S(2)}, u32[]{:S(2)}) collective-permute-start(f32[1,8,256]{2,1,0:T(8,128)S(1)} %get-tuple-element.120), channel_id=1, source_target_pairs={{16,0},{32,16},{48,32},{64,48},{80,64},{96,80},{112,96},{128,112},... | collective-permute-start | bytes 24584 | tf_op jit(solution)/shard_map/ppermute | solution.py:24
  431.6 7.7 %collective-permute-start.45 = (f32[1,8,256]{2,1,0:T(8,128)S(1)}, f32[1,8,256]{2,1,0:T(8,128)S(1)}, u32[]{:S(2)}, u32[]{:S(2)}) collective-permute-start(f32[1,8,256]{2,1,0:T(8,128)S(1)} %get-tuple-element.119), channel_id=1, source_target_pairs={{0,16},{16,32},{32,48},{48,64},{64,80},{80,96},{96,112},{112,128},... | collective-permute-start | bytes 24584 | tf_op jit(solution)/shard_map/ppermute | solution.py:21
  442.5 5.4 collective-permute-start.48
  444.5 7.7 %collective-permute-start.49 = (f32[1,8,256]{2,1,0:T(8,128)S(1)}, f32[1,8,256]{2,1,0:T(8,128)S(1)}, u32[]{:S(2)}, u32[]{:S(2)}) collective-permute-start(f32[1,8,256]{2,1,0:T(8,128)S(1)} %get-tuple-element.113), channel_id=1, source_target_pairs={{0,16},{16,32},{32,48},{48,64},{64,80},{80,96},{96,112},{112,128},... | collective-permute-start | bytes 24584 | tf_op jit(solution)/shard_map/ppermute | solution.py:21
  457.5 5.4 collective-permute-start.52
  459.4 7.7 %collective-permute-start.53 = (f32[1,8,256]{2,1,0:T(8,128)S(1)}, f32[1,8,256]{2,1,0:T(8,128)S(1)}, u32[]{:S(2)}, u32[]{:S(2)}) collective-permute-start(f32[1,8,256]{2,1,0:T(8,128)S(1)} %get-tuple-element.107), channel_id=1, source_target_pairs={{0,16},{16,32},{32,48},{48,64},{64,80},{80,96},{96,112},{112,128},... | collective-permute-start | bytes 24584 | tf_op jit(solution)/shard_map/ppermute | solution.py:21
  472.7 5.6 %collective-permute-start.56 = (f32[1,8,256]{2,1,0:T(8,128)S(1)}, f32[1,8,256]{2,1,0:T(8,128)S(1)}, u32[]{:S(2)}, u32[]{:S(2)}) collective-permute-start(f32[1,8,256]{2,1,0:T(8,128)S(1)} %get-tuple-element.102), channel_id=1, source_target_pairs={{16,0},{32,16},{48,32},{64,48},{80,64},{96,80},{112,96},{128,112},... | collective-permute-start | bytes 24584 | tf_op jit(solution)/shard_map/ppermute | solution.py:24
  474.6 7.9 %collective-permute-start.57 = (f32[1,8,256]{2,1,0:T(8,128)S(1)}, f32[1,8,256]{2,1,0:T(8,128)S(1)}, u32[]{:S(2)}, u32[]{:S(2)}) collective-permute-start(f32[1,8,256]{2,1,0:T(8,128)S(1)} %get-tuple-element.101), channel_id=1, source_target_pairs={{0,16},{16,32},{32,48},{48,64},{64,80},{80,96},{96,112},{112,128},... | collective-permute-start | bytes 24584 | tf_op jit(solution)/shard_map/ppermute | solution.py:21
  492.4 5.4 collective-permute-start.60
  494.3 8.0 %collective-permute-start.61 = (f32[1,16,512]{2,1,0:T(8,128)S(1)}, f32[1,16,512]{2,1,0:T(8,128)S(1)}, u32[]{:S(2)}, u32[]{:S(2)}) collective-permute-start(f32[1,16,512]{2,1,0:T(8,128)S(1)} %get-tuple-element.50), channel_id=1, source_target_pairs={{0,16},{16,32},{32,48},{48,64},{64,80},{80,96},{96,112},{112,128},... | collective-permute-start | bytes 98312 | tf_op jit(solution)/shard_map/ppermute | solution.py:21
  508.3 5.4 collective-permute-start.64
  510.2 8.0 %collective-permute-start.65 = (f32[1,16,512]{2,1,0:T(8,128)S(1)}, f32[1,16,512]{2,1,0:T(8,128)S(1)}, u32[]{:S(2)}, u32[]{:S(2)}) collective-permute-start(f32[1,16,512]{2,1,0:T(8,128)S(1)} %get-tuple-element.44), channel_id=1, source_target_pairs={{0,16},{16,32},{32,48},{48,64},{64,80},{80,96},{96,112},{112,128},... | collective-permute-start | bytes 98312 | tf_op jit(solution)/shard_map/ppermute | solution.py:21
  518.2 5.3 collective-permute-start.66
  524.3 5.4 collective-permute-start.68
  526.3 8.0 %collective-permute-start.69 = (f32[1,16,512]{2,1,0:T(8,128)S(1)}, f32[1,16,512]{2,1,0:T(8,128)S(1)}, u32[]{:S(2)}, u32[]{:S(2)}) collective-permute-start(f32[1,16,512]{2,1,0:T(8,128)S(1)} %get-tuple-element.38), channel_id=1, source_target_pairs={{0,16},{16,32},{32,48},{48,64},{64,80},{80,96},{96,112},{112,128},... | collective-permute-start | bytes 98312 | tf_op jit(solution)/shard_map/ppermute | solution.py:21
  534.3 5.3 collective-permute-start.70
  540.4 5.4 collective-permute-start.72
  542.3 8.0 %collective-permute-start.73 = (f32[1,16,512]{2,1,0:T(8,128)S(1)}, f32[1,16,512]{2,1,0:T(8,128)S(1)}, u32[]{:S(2)}, u32[]{:S(2)}) collective-permute-start(f32[1,16,512]{2,1,0:T(8,128)S(1)} %get-tuple-element.32), channel_id=1, source_target_pairs={{0,16},{16,32},{32,48},{48,64},{64,80},{80,96},{96,112},{112,128},... | collective-permute-start | bytes 98312 | tf_op jit(solution)/shard_map/ppermute | solution.py:21
  (29 other events, 213.3 us)
where the time goes:
time: 559 us; the launch traced here: 557 us
  blocking collectives  210 us (38%)
  starting transfers between devices  186 us (33%)
  waiting for transfers between devices  90.3 us (16%)
  local copies, waits for them, and re-layouts  49.4 us (9%)
  other arithmetic  16.7 us (3%)
    ppermute x36, starting transfers between devices, with_halo(): lax.ppermute(lax.slice_in_dim(block, 0, width, axis=dim), axis, backward)  119 us
    psum x1, blocking collectives, shards(): lax.psum(jnp.sum(coarsest, axis=(1, 2, 3)), ('gx', 'gy')) / cell_count  102 us
    ppermute x36, waiting for transfers between devices, with_halo(): lax.ppermute(lax.slice_in_dim(block, block.shape[dim] - width, None, axis...  77.7 us
    all_gather x2, blocking collectives, along_rows(): lax.all_gather(values, 'gx', axis=0, tiled=True)  57.5 us
    ppermute x36, starting transfers between devices, with_halo(): lax.ppermute(lax.slice_in_dim(block, block.shape[dim] - width, None, axis...  57.1 us
    all_gather x2, blocking collectives, along_cols(): lax.all_gather(values, 'gy', axis=1, tiled=True)  50.3 us
    reshape x2, local copies, waits for them, and re-layouts, restrict(): residual.reshape(dims[0] // 2, 2, dims[1] // 2, 2, dims[2] // 2, 2)  21.5 us
    ppermute x36, waiting for transfers between devices, with_halo(): lax.ppermute(lax.slice_in_dim(block, 0, width, axis=dim), axis, backward)  12.6 us
  transfers between devices with their start and end apart: 76, of which 47 were waited for; matrix products, arithmetic and copies ran while one was open for 9% of the time, Pallas kernels for 0%

commit v1 on v0

v1 whole, which is shorter than its diff:
```python
import functools

import jax
import jax.numpy as jnp
import numpy as np
from jax import lax
from jax.experimental import pallas as pl
from jax.experimental.pallas import tpu as pltpu
from jax.sharding import PartitionSpec as P

MASS = 0.002
LX, LY = 8, 16
LANES = 128
MESH = pl.DeviceIdType.MESH
F32 = jnp.float32


def cas(rows, cols, length):
    angle = 2.0 * np.pi * ((rows * cols) % length) / length
    return np.cos(angle) + np.sin(angle)


@functools.lru_cache(maxsize=4)
def tables(gxn, gyn):
    nx, ny = 2 * gxn, 4 * gyn
    lanes = np.arange(LANES)
    depth = cas(lanes[:, None], lanes[None, :], LANES)
    rows = np.arange(nx)
    along_x = np.kron(cas(rows[:, None], rows[None, :], nx), np.eye(4))
    padded = along_x[(np.arange(4 * nx + 16) - 8) % (4 * nx)]
    cols = np.arange(ny)
    first = np.zeros((gyn, 2, 4, gyn, 2, 4))
    last = np.zeros((gyn, 6, 8, gyn, 6, 4))
    for me in range(gyn):
        table = cas((4 * me + np.arange(4))[:, None], cols[None, :], ny).reshape(4, gyn, 4)
        for i in range(2):
            first[me, i, :, :, i, :] = table
        table = cas(((4 * me - 2 + np.arange(8)) % ny)[:, None], cols[None, :], ny).reshape(8, gyn, 4)
        for i in range(6):
            last[me, i, :, :, i, :] = table
    first = first.reshape(gyn, 8, gyn * 8)
    last = last.reshape(gyn, 48, gyn * 24)
    wave_x = np.repeat(2.0 - 2.0 * np.cos(2.0 * np.pi * rows / nx), 4)[:, None] * np.ones((1, LANES))
    ky = 4 * np.arange(gyn)[:, None] + np.tile(np.arange(4), 2)[None, :]
    wave_y = (2.0 - 2.0 * np.cos(2.0 * np.pi * ky / ny))[:, :, None] * np.ones((1, 1, LANES))
    wave_z = (2.0 - 2.0 * np.cos(2.0 * np.pi * lanes / LANES))[None, :] * np.ones((8, 1))
    pick = np.zeros((4 * LANES, 4 * LANES))
    column = np.arange(4 * LANES)
    pick[4 * (column % LANES) + column // LANES, column] = 1.0
    out = [np.asarray(t, np.float32) for t in (depth, padded, first, last, wave_x, wave_y, wave_z)]
    return out + [pick.astype(jnp.bfloat16)]


def permuted(values, pick, dims):
    total = None
    rest = values
    for _ in range(3):
        part = rest.astype(jnp.bfloat16)
        rest = rest - part.astype(F32)
        term = lax.dot_general(part, pick, (dims, ((), ())), preferred_element_type=F32)
        total = term if total is None else total + term
    return total


def dot(a, b):
    return lax.dot_general(
        a, b, (((1,), (0,)), ((), ())), precision=lax.Precision.HIGHEST, preferred_element_type=F32
    )


def kernel(
    gxn,
    gyn,
    src_ref,
    coef_ref,
    depth_ref,
    alongx_ref,
    first_ref,
    last_ref,
    wavex_ref,
    wavey_ref,
    wavez_ref,
    pick_ref,
    out_ref,
    W,
    V,
    C,
    G,
    DG,
    T,
    W1,
    D1,
    I1,
    C1,
    B1,
    V1,
    VB,
    T1,
    Z,
    G1,
    G2,
    G3,
    DI,
    S1,
    S2,
    CR,
    Q,
    M3,
    face_s,
    face_r,
    blk_s,
    blk_r,
    g1_s,
    g1_r,
    g2_s,
    g2_r,
    g3_s,
    g3_r,
    c1_s,
    c1_r,
    c2_s,
    c2_r,
    m_sem,
):
    gx = lax.axis_index("gx")
    gy = lax.axis_index("gy")

    def at(dx, dy):
        return (lax.rem(gx + dx + gxn, gxn), lax.rem(gy + dy + gyn, gyn))

    around = [(dx, dy) for dx in (-1, 0, 1) for dy in (-1, 0, 1) if (dx, dy) != (0, 0)]

    barrier = pltpu.get_barrier_semaphore()
    for dx, dy in around:
        if dx and dy:
            pl.semaphore_signal(barrier, inc=1, device_id=at(dx, dy), device_id_type=MESH)

    def greet_x(i, carry):
        pl.semaphore_signal(barrier, inc=1, device_id=(lax.rem(gx + 1 + i, gxn), gy), device_id_type=MESH)
        return carry

    def greet_y(i, carry):
        pl.semaphore_signal(barrier, inc=1, device_id=(gx, lax.rem(gy + 1 + i, gyn)), device_id_type=MESH)
        return carry

    lax.fori_loop(0, gxn - 1, greet_x, 0)
    lax.fori_loop(0, gyn - 1, greet_y, 0)

    m3_copy = pltpu.make_async_copy(last_ref.at[gy], M3, m_sem)
    m3_copy.start()

    def remote(src, dst, ssem, rsem, dev):
        return pltpu.make_async_remote_copy(
            src_ref=src, dst_ref=dst, send_sem=ssem, recv_sem=rsem, device_id=dev, device_id_type=MESH
        )

    def start(copies):
        for copy in copies:
            copy.start()

    def wait(copies):
        for copy in copies:
            copy.wait()

    def faces(c, k):
        own = pl.ds(8, 2 * LY)
        ends = (
            (V.at[c, LX, own], V.at[c, 0, own], (1, 0)),
            (V.at[c, 1, own], V.at[c, LX + 1, own], (-1, 0)),
            (V.at[c, pl.ds(1, LX), pl.ds(32, 8)], V.at[c, pl.ds(1, LX), pl.ds(0, 8)], (0, 1)),
            (V.at[c, pl.ds(1, LX), pl.ds(8, 8)], V.at[c, pl.ds(1, LX), pl.ds(40, 8)], (0, -1)),
        )
        return [remote(s, d, face_s.at[k, i], face_r.at[k, i], at(*to)) for i, (s, d, to) in enumerate(ends)]

    def blocks(src, dst, k):
        copies = []
        for i, (dx, dy) in enumerate(around):
            there = dst.at[:, pl.ds(4 - 4 * dx, 4), pl.ds(16 - 8 * dy, 8)]
            copies.append(
                remote(src.at[:, pl.ds(4, 4), pl.ds(16, 8)], there, blk_s.at[k, i], blk_r.at[k, i], at(dx, dy))
            )
        return copies

    def gather(ref, along_gx, ssem, rsem):
        me, count = (gx, gxn) if along_gx else (gy, gyn)

        def peer(i):
            return lax.rem(me + 1 + i, count)

        def send(i, carry):
            dev = (peer(i), gy) if along_gx else (gx, peer(i))
            remote(ref.at[me], ref.at[me], ssem.at[i], rsem.at[me], dev).start()
            return carry

        def finish():
            def take(i, carry):
                dev = (peer(i), gy) if along_gx else (gx, peer(i))
                copy = remote(ref.at[me], ref.at[peer(i)], ssem.at[i], rsem.at[peer(i)], dev)
                copy.wait_send()
                copy.wait_recv()
                return carry

            lax.fori_loop(0, count - 1, take, 0)

        lax.fori_loop(0, count - 1, send, 0)
        return finish

    def iota(shape, dim):
        return lax.broadcasted_iota(jnp.int32, shape, dim)

    def spread(values, x, put):
        even = ((iota((LY, LANES), 0) + x) & 1) == 0
        for h in (0, 1):
            a = values[:, 2 * h * LANES : (2 * h + 1) * LANES]
            b = values[:, (2 * h + 1) * LANES : (2 * h + 2) * LANES]
            put(0, h, jnp.where(even, a, b))
            put(1, h, jnp.where(even, b, a))

    for d in range(3):
        flat = coef_ref[d].reshape(LX * LY, 4 * LANES)
        mixed = lax.dot_general(flat, pick_ref[...], (((1,), (0,)), ((), ())), preferred_element_type=F32)
        for x in range(LX):

            def put(c, h, values, d=d, x=x):
                W[2 * d + c, x + 1, pl.ds(8 + h, LY, stride=2), :] = values

            spread(mixed[x * LY : (x + 1) * LY], x, put)

    pl.semaphore_wait(barrier, gxn - 1 + gyn - 1 + 4)

    back = [
        remote(
            W.at[pl.ds(0, 2), LX, pl.ds(8, 2 * LY)],
            W.at[pl.ds(0, 2), 0, pl.ds(8, 2 * LY)],
            face_s.at[8, 0],
            face_r.at[8, 0],
            at(1, 0),
        ),
        remote(
            W.at[pl.ds(2, 2), pl.ds(1, LX), pl.ds(32, 8)],
            W.at[pl.ds(2, 2), pl.ds(1, LX), pl.ds(0, 8)],
            face_s.at[8, 1],
            face_r.at[8, 1],
            at(0, 1),
        ),
    ]
    start(back)

    mixed = permuted(src_ref[...].reshape(LX * LY, 4 * LANES), pick_ref[...], ((1,), (0,)))
    for x in range(LX):

        def put(c, h, values, x=x):
            G[c, x, pl.ds(h, LY, stride=2), :] = values

        spread(mixed[x * LY : (x + 1) * LY], x, put)

    own = pl.ds(8, 2 * LY)
    s32 = iota((2 * LY, LANES), 0)
    h_zero = (s32 & 1) == 0
    y_par = (s32 >> 1) & 1
    j8 = iota((8, LANES), 0)

    def pairs(i, values):
        T[i] = values
        return [T[i, pl.ds(h, 8, stride=4), :] + T[i, pl.ds(h + 2, 8, stride=4), :] for h in (0, 1)]

    def colours(i, two, scale):
        even = ((j8 + i) & 1) == 0
        return jnp.where(even, two[0], two[1]) * scale, jnp.where(even, two[1], two[0]) * scale

    def coarsen(i, carry):
        lo, hi = 1 + 2 * i, 2 + 2 * i
        mine = pl.ds(16, 8)
        e, o = colours(i, pairs(i, W[0, hi, own] + W[1, hi, own]), 0.0625)
        W1[0, 4 + i, mine] = e
        W1[1, 4 + i, mine] = o
        T[i] = W[2, lo, own] + W[3, lo, own] + W[2, hi, own] + W[3, hi, own]
        e, o = colours(i, [T[i, pl.ds(2 + h, 8, stride=4), :] for h in (0, 1)], 0.0625)
        W1[2, 4 + i, mine] = e
        W1[3, 4 + i, mine] = o
        even = y_par == 0
        low = jnp.where(even, W[5, lo, own], W[4, lo, own])
        e, o = colours(i, pairs(i, low + jnp.where(even, W[4, hi, own], W[5, hi, own])), 0.0625)
        W1[4, 4 + i, mine] = e
        W1[5, 4 + i, mine] = o
        return carry

    lax.fori_loop(0, 4, coarsen, 0)
    w1_copies = blocks(W1, W1, 0)

    def other(read, c, parity):
        pc0 = y_par == (parity ^ c)
        up, down = read(1), read(-1)
        return jnp.where(
            h_zero,
            jnp.where(pc0, pltpu.roll(up, 1, 1), up),
            jnp.where(pc0, down, pltpu.roll(down, LANES - 1, 1)),
        )

    def coefficients(i, carry):
        for parity in (0, 1):
            x = 2 * i + parity
            for c in (0, 1):
                o = 1 - c
                pc0 = y_par == (parity ^ c)
                xp, xm = W[c, x + 1, own], W[o, x, own]
                yp, ym = W[2 + c, x + 1, own], W[2 + o, x + 1, pl.ds(6, 2 * LY)]
                zc, zo = W[4 + c, x + 1, own], W[4 + o, x + 1, own]
                zs = jnp.where(pc0, zc, zo)
                far = other(lambda ds: W[4 + o, x + 1, pl.ds(8 + ds, 2 * LY)], c, parity)
                zt = jnp.where(pc0, far, zc)
                diagonal = MASS + xp + xm + yp + ym + zs + zt
                inverse = 1.0 / diagonal
                for k, value in enumerate((xp, xm, yp, ym, zs, zt)):
                    C[c, k, x] = value * inverse
                DG[c, x] = diagonal
                G[c, x] = G[c, x] * inverse
                if c == 0:
                    V[0, x + 1, own] = G[0, x]
        return carry

    def weighted(c, x, parity):
        o = 1 - c
        total = G[c, x] + C[c, 0, x] * V[o, x + 2, own] + C[c, 1, x] * V[o, x, own]
        total = total + C[c, 2, x] * V[o, x + 1, pl.ds(10, 2 * LY)] + C[c, 3, x] * V[o, x + 1, pl.ds(6, 2 * LY)]
        far = other(lambda ds: V[o, x + 1, pl.ds(8 + ds, 2 * LY)], c, parity)
        return total + C[c, 4, x] * V[o, x + 1, own] + C[c, 5, x] * far

    def half_sweep(c):
        def rows(i, carry):
            for parity in (0, 1):
                x = 2 * i + parity
                V[c, x + 1, own] = weighted(c, x, parity)
            return carry

        lax.fori_loop(0, LX // 2, rows, 0)

    wait(back)
    lax.fori_loop(0, LX // 2, coefficients, 0)
    copies = faces(0, 0)
    start(copies)
    start(w1_copies)

    sums = []
    mine = pl.ds(16, 8)
    sums.append(W1[0, 5, mine] + W1[1, 5, mine] + W1[0, 7, mine] + W1[1, 7, mine])
    part_y, part_z = 0.0, 0.0
    for i in range(4):
        part_y = part_y + jnp.where((j8 & 1) == 1, W1[2, 4 + i, mine] + W1[3, 4 + i, mine], 0.0)
        part_z = part_z + jnp.where(((j8 + i) & 1) == 0, W1[5, 4 + i, mine], W1[4, 4 + i, mine])
    sums += [part_y, part_z]
    scale = 1.0 / (16.0 * 2 * gxn * 4 * gyn * LANES)
    lane = iota((1, LANES), 1)
    row = jnp.zeros((1, LANES), F32)
    for d in range(3):
        value = jnp.sum(jnp.sum(sums[d], axis=0, keepdims=True), axis=1, keepdims=True)
        row = row + jnp.where(lane == d, value * scale, 0.0)
    S1[gy] = row
    wait_c1 = gather(S1, False, c1_s, c1_r)

    wait(copies)
    half_sweep(1)
    copies = faces(1, 1)
    start(copies)

    wait(w1_copies)

    def z_terms(c, x, sub, parity_iota):
        o = 1 - c
        pc0 = ((parity_iota + x + c) & 1) == 0
        zc, zo = W1[4 + c, x, sub], W1[4 + o, x, sub]
        return jnp.where(pc0, zc, zo), jnp.where(pc0, pltpu.roll(zo, 1, 1), zc)

    def diagonals(i, carry):
        x = 4 + i
        for c in (0, 1):
            o = 1 - c
            zs, zt = z_terms(c, x, pl.ds(16, 8), j8)
            total = MASS + W1[c, x, pl.ds(16, 8)] + W1[o, x - 1, pl.ds(16, 8)]
            total = total + W1[2 + c, x, pl.ds(16, 8)] + W1[2 + o, x, pl.ds(15, 8)]
            D1[c, x, pl.ds(16, 8)] = total + zs + zt
        return carry

    lax.fori_loop(0, 4, diagonals, 0)
    d1_copies = blocks(D1, D1, 1)
    start(d1_copies)

    wait(copies)
    half_sweep(0)
    copies = faces(0, 2)
    start(copies)

    wait_c1()
    S2[gx] = jnp.sum(S1[...], axis=0)
    wait_c2 = gather(S2, True, c2_s, c2_r)

    wait(copies)
    half_sweep(1)
    copies = faces(1, 3)
    start(copies)

    wait(d1_copies)
    wide = pl.ds(8, 24)
    s24 = iota((24, LANES), 0)

    def inverses(x, carry):
        for c in (0, 1):
            I1[c, x] = 1.0 / D1[c, x, wide]
        return carry

    lax.fori_loop(0, 12, inverses, 0)

    def coefficients1(i, carry):
        x = 1 + i
        for c in (0, 1):
            o = 1 - c
            inverse = I1[c, x]
            zs, zt = z_terms(c, x, wide, s24)
            values = (W1[c, x, wide], W1[o, x - 1, wide], W1[2 + c, x, wide], W1[2 + o, x, pl.ds(7, 24)], zs, zt)
            for k, value in enumerate(values):
                C1[c, k, x] = value * inverse
        return carry

    lax.fori_loop(0, 10, coefficients1, 0)

    wait(copies)

    def restrict(i, carry):
        total = None
        for parity in (0, 1):
            x = 2 * i + parity
            for c in (0, 1):
                r = DG[c, x] * (weighted(c, x, parity) - V[c, x + 1, own])
                total = r if total is None else total + r
        e, o = colours(i, pairs(i, total), 0.125)
        B1[0, 4 + i, pl.ds(16, 8)] = e
        B1[1, 4 + i, pl.ds(16, 8)] = o
        return carry

    lax.fori_loop(0, 4, restrict, 0)
    copies = blocks(B1, B1, 2)
    start(copies)

    wait_c2()
    CR[...] = jnp.sum(S2[...], axis=0)
    mean = [jnp.sum(jnp.where(lane == d, CR[...], 0.0), axis=1, keepdims=True) for d in range(3)]
    cells = float(2 * gxn * 4 * gyn * LANES)
    flat_part = MASS + mean[1] * wavey_ref[gy] + mean[2] * wavez_ref[...]

    def eigen(i, carry):
        tile = pl.ds(pl.multiple_of(8 * i, 8), 8)
        DI[tile, :] = 1.0 / ((flat_part + mean[0] * wavex_ref[tile, :]) * cells)
        return carry

    lax.fori_loop(0, gxn, eigen, 0)

    def weighted1(A, c, x):
        o = 1 - c
        pc0 = ((s24 + x + c) & 1) == 0
        here = A[o, x, wide]
        total = B1[c, x, wide] * I1[c, x] + C1[c, 0, x] * A[o, x + 1, wide] + C1[c, 1, x] * A[o, x - 1, wide]
        total = total + C1[c, 2, x] * A[o, x, pl.ds(9, 24)] + C1[c, 3, x] * A[o, x, pl.ds(7, 24)]
        far = jnp.where(pc0, pltpu.roll(here, 1, 1), pltpu.roll(here, LANES - 1, 1))
        return total + C1[c, 4, x] * here + C1[c, 5, x] * far

    def half_sweep1(A, c, low):
        def rows(i, carry):
            x = low + i
            A[c, x, wide] = weighted1(A, c, x)
            return carry

        lax.fori_loop(0, 12 - 2 * low, rows, 0)

    wait(copies)

    def first1(x, carry):
        V1[0, x, wide] = B1[0, x, wide] * I1[0, x]
        return carry

    lax.fori_loop(0, 12, first1, 0)
    half_sweep1(V1, 1, 1)
    half_sweep1(V1, 0, 2)
    half_sweep1(V1, 1, 3)

    for i in range(2):
        total = None
        for k in range(2):
            x = 4 + 2 * i + k
            for c in (0, 1):
                r = (weighted1(V1, c, x) - V1[c, x, wide])[8:16] * D1[c, x, pl.ds(16, 8)]
                total = r if total is None else total + r
        T1[pl.ds(8, 8), :] = total
        Z[pl.ds(4 * i, 4), :] = (T1[pl.ds(8, 4, stride=2), :] + T1[pl.ds(9, 4, stride=2), :]) * 0.125

    G1[gy] = dot(Z[...], depth_ref[...])
    finish = gather(G1, False, g1_s, g1_r)
    v1_copies = blocks(V1, VB, 3)
    start(v1_copies)
    VB[:, pl.ds(4, 4), pl.ds(16, 8)] = V1[:, pl.ds(4, 4), pl.ds(16, 8)]
    finish()
    G2[gx] = dot(first_ref[gy], G1[...].reshape(8 * gyn, LANES))
    finish = gather(G2, True, g2_s, g2_r)
    finish()
    spectrum = dot(alongx_ref[pl.ds(8, 8 * gxn), :], G2[...].reshape(8 * gxn, LANES)) * DI[...]
    back_x = dot(alongx_ref[pl.ds(pl.multiple_of(8 * gx, 8), 24), :], spectrum)
    G3[gy] = dot(back_x, depth_ref[...])
    finish = gather(G3, False, g3_s, g3_r)
    m3_copy.wait()
    wait(v1_copies)
    finish()
    coarse = dot(M3[...], G3[...].reshape(24 * gyn, LANES))

    for a in range(6):
        part = coarse[8 * a : 8 * a + 8]
        T1[pl.ds(4, 8, stride=2), :] = part
        T1[pl.ds(5, 8, stride=2), :] = part
        for x in (2 * a, 2 * a + 1):
            for c in (0, 1):
                VB[c, x, wide] = VB[c, x, wide] + T1[...]
    half_sweep1(VB, 0, 1)
    half_sweep1(VB, 1, 2)
    half_sweep1(VB, 0, 3)
    half_sweep1(VB, 1, 4)

    def prolong(i, carry):
        even = ((j8 + i) & 1) == 0
        e, o = VB[0, 4 + i, pl.ds(16, 8)], VB[1, 4 + i, pl.ds(16, 8)]
        for h, part in enumerate((jnp.where(even, e, o), jnp.where(even, o, e))):
            T[i, pl.ds(h, 8, stride=4), :] = part
            T[i, pl.ds(h + 2, 8, stride=4), :] = part
        for x in (2 * i, 2 * i + 1):
            for c in (0, 1):
                V[c, x + 1, own] = V[c, x + 1, own] + T[i]
        return carry

    lax.fori_loop(0, 4, prolong, 0)
    for k, c in enumerate((1, 0, 1, 0)):
        copies = faces(c, 4 + k)
        start(copies)
        wait(copies)
        half_sweep(1 - c)

    for x in range(LX):
        even = ((iota((LY, LANES), 0) + x) & 1) == 0
        for h in (0, 1):
            e, o = V[0, x + 1, pl.ds(8 + h, LY, stride=2), :], V[1, x + 1, pl.ds(8 + h, LY, stride=2), :]
            rows = pl.ds(x * LY, LY)
            Q[rows, pl.ds(2 * h * LANES, LANES)] = jnp.where(even, e, o)
            Q[rows, pl.ds((2 * h + 1) * LANES, LANES)] = jnp.where(even, o, e)
    out_ref[...] = permuted(Q[...], pick_ref[...], ((1,), (1,))).reshape(LX, LY, 4 * LANES)


def solution(mesh):
    gxn, gyn = mesh.shape["gx"], mesh.shape["gy"]
    consts = tables(gxn, gyn)

    def step(source, face_coef):
        vmem = pl.BlockSpec(memory_space=pltpu.VMEM)
        dma = pltpu.SemaphoreType.DMA
        V = pltpu.VMEM
        return pl.pallas_call(
            functools.partial(kernel, gxn, gyn),
            out_shape=jax.ShapeDtypeStruct((LX, LY, 4 * LANES), F32),
            in_specs=[vmem] * 5 + [pl.BlockSpec(memory_space=pl.ANY)] + [vmem] * 4,
            out_specs=vmem,
            scratch_shapes=[
                V((6, LX + 2, 48, LANES), F32),
                V((2, LX + 2, 48, LANES), F32),
                V((2, 6, LX, 32, LANES), F32),
                V((2, LX, 32, LANES), F32),
                V((2, LX, 32, LANES), F32),
                V((4, 32, LANES), F32),
                V((6, 12, 40, LANES), F32),
                V((2, 12, 40, LANES), F32),
                V((2, 12, 24, LANES), F32),
                V((2, 6, 12, 24, LANES), F32),
                V((2, 12, 40, LANES), F32),
                V((2, 12, 40, LANES), F32),
                V((2, 12, 40, LANES), F32),
                V((24, LANES), F32),
                V((8, LANES), F32),
                V((gyn, 8, LANES), F32),
                V((gxn, 8, LANES), F32),
                V((gyn, 24, LANES), F32),
                V((8 * gxn, LANES), F32),
                V((gyn, 1, LANES), F32),
                V((gxn, 1, LANES), F32),
                V((1, LANES), F32),
                V((LX * LY, 4 * LANES), F32),
                V((48, 24 * gyn), F32),
                dma((9, 4)),
                dma((9, 4)),
                dma((4, 8)),
                dma((4, 8)),
                dma((gyn,)),
                dma((gyn,)),
                dma((gxn,)),
                dma((gxn,)),
                dma((gyn,)),
                dma((gyn,)),
                dma((gyn,)),
                dma((gyn,)),
                dma((gxn,)),
                dma((gxn,)),
                dma,
            ],
            compiler_params=pltpu.CompilerParams(
                collective_id=0, has_side_effects=True, vmem_limit_bytes=60 * 1024 * 1024
            ),
            name="cycle",
        )(source, face_coef, *[jnp.asarray(t) for t in consts])

    return jax.shard_map(
        step,
        mesh=mesh,
        in_specs=(P("gx", "gy", None), P(None, "gx", "gy", None)),
        out_specs=P("gx", "gy", None),
        check_vma=False,
    )
```

time: 559 us -> 95.6 us (0.17)
  blocking collectives: 210 us -> 0 us
  starting transfers between devices: 186 us -> 0 us
  Pallas kernels: 0 us -> 93.7 us
  waiting for transfers between devices: 90.3 us -> 0 us
  local copies, waits for them, and re-layouts: 49.4 us -> 1.67 us
  other arithmetic: 16.7 us -> 0 us
    ppermute x76 -> x0, starting transfers between devices: 186 us -> none  [the longest x36 119 us: with_halo(): lax.ppermute(lax.slice_in_dim(block, 0, width, axis=dim), axis, backward)]
    all_gather x4 -> x0, blocking collectives: 108 us -> none  [the longest x2 57.5 us: along_rows(): lax.all_gather(values, 'gx', axis=0, tiled=True)]
    psum x1 -> x0, blocking collectives: 102 us -> none  [shards(): lax.psum(jnp.sum(coarsest, axis=(1, 2, 3)), ('gx', 'gy')) / cell_count]
    pallas_call x0 -> x1, Pallas kernels: none -> 93.7 us  [step(): pl.pallas_call(functools.partial(kernel, gxn, gyn), out_shape=jax.ShapeDt...]
    ppermute x76 -> x0, waiting for transfers between devices: 90.3 us -> none  [the longest x36 77.7 us: with_halo(): lax.ppermute(lax.slice_in_dim(block, block.shape[dim] - width, None, axis...]
    reshape x7 -> x0, local copies, waits for them, and re-layouts: 24.4 us -> none  [the longest x2 21.5 us: restrict(): residual.reshape(dims[0] // 2, 2, dims[1] // 2, 2, dims[2] // 2, 2)]
    slice x90 -> x0, local copies, waits for them, and re-layouts: 23.1 us -> none  [the longest x2 5.09 us: coarsen(): upper_face = couplings[2][:, :, 1::2]]
    reduce_sum x3 -> x0, other arithmetic: 8.9 us -> none  [the longest x2 8.79 us: restrict(): residual.reshape(dims[0] // 2, 2, dims[1] // 2, 2, dims[2] // 2, 2)]
  transfers between devices with their start and end apart: 76 -> 0, of which waited for: 47 -> 0; matrix products, arithmetic and copies ran while one was open for 9% -> 0% of each run, Pallas kernels for 0% -> 0%
where the time goes in v1:
time: 95.6 us; the launch traced here: 95.4 us
  Pallas kernels  93.7 us (98%)
  local copies, waits for them, and re-layouts  1.67 us (2%)
    pallas_call x1, Pallas kernels, step(): pl.pallas_call(functools.partial(kernel, gxn, gyn), out_shape=jax.ShapeDt...  93.7 us

profile of v1, /device:TPU:1, one launch (start us, length us, event | category | flops | bytes accessed | tf_op | source)
XLA Modules:
  0.0 95.4 jit_solution(16400965269461710853)
XLA Ops:
  0.0 93.7 %cycle.1 = f32[8,16,512]{2,1,0:T(8,128)} custom-call(f32[8,16,512]{2,1,0:T(8,128)} %src_ref.1, bf16[3,8,16,512]{3,2,1,0:T(8,128)(2,1)} %coef_ref.1, f32[128,128]{1,0:T(8,128)} %constant.16.clone.depth_ref, f32[272,256]{1,0:T(8,128)} %constant.17.clone.alongx_ref, f32[16,8,128]{2,1,0:T(8,128)} %constant.18.clone.first_ref, ...), custom_call_target="tpu_custom_call" | custom-call | tf_op jit(solution)/shard_map/cycle/pallas_call | solution.py:561
  93.7 1.7 %copy.12 = f32[8,16,512]{2,1,0:T(8,128)} copy(f32[8,16,512]{2,1,0:T(8,128)} %cycle.1) | data formatting | bytes 524288

commit v2 on v1

v2 whole, which is shorter than its diff:
```python
import functools

import jax
import jax.numpy as jnp
import numpy as np
from jax import lax
from jax.experimental import pallas as pl
from jax.experimental.pallas import tpu as pltpu
from jax.sharding import PartitionSpec as P

MASS = 0.002
LX, LY = 8, 16
LANES = 128
MESH = pl.DeviceIdType.MESH
F32 = jnp.float32


def cas(rows, cols, length):
    angle = 2.0 * np.pi * ((rows * cols) % length) / length
    return np.cos(angle) + np.sin(angle)


@functools.lru_cache(maxsize=4)
def tables(gxn, gyn):
    nx, ny = 2 * gxn, 4 * gyn
    lanes = np.arange(LANES)
    depth = cas(lanes[:, None], lanes[None, :], LANES)
    rows = np.arange(nx)
    along_x = np.kron(cas(rows[:, None], rows[None, :], nx), np.eye(4))
    padded = along_x[(np.arange(4 * nx + 24) - 12) % (4 * nx)]
    cols = np.arange(ny)
    first = np.zeros((gyn, 2, 4, gyn, 2, 4))
    last = np.zeros((gyn, 16, gyn, 8, 4))
    for me in range(gyn):
        table = cas((4 * me + np.arange(4))[:, None], cols[None, :], ny).reshape(4, gyn, 4)
        for i in range(2):
            first[me, i, :, :, i, :] = table
        table = cas(((4 * me - 3 + np.arange(16)) % ny)[:, None], cols[None, :], ny).reshape(16, gyn, 4)
        last[me] = table[:, :, None, :]
    first = first.reshape(gyn, 8, gyn * 8)
    last = last.reshape(gyn, 16, gyn * 32)
    wave_x = np.repeat(2.0 - 2.0 * np.cos(2.0 * np.pi * rows / nx), 4)[:, None] * np.ones((1, LANES))
    ky = 4 * np.arange(gyn)[:, None] + np.tile(np.arange(4), 2)[None, :]
    wave_y = (2.0 - 2.0 * np.cos(2.0 * np.pi * ky / ny))[:, :, None] * np.ones((1, 1, LANES))
    wave_z = (2.0 - 2.0 * np.cos(2.0 * np.pi * lanes / LANES))[None, :] * np.ones((8, 1))
    pick = np.zeros((4 * LANES, 4 * LANES))
    column = np.arange(4 * LANES)
    pick[4 * (column % LANES) + column // LANES, column] = 1.0
    out = [np.asarray(t, np.float32) for t in (depth, along_x, padded, first, last, wave_x, wave_y, wave_z)]
    return out + [pick.astype(jnp.bfloat16)]


def permuted(values, pick, dims):
    total = None
    rest = values
    for _ in range(3):
        part = rest.astype(jnp.bfloat16)
        rest = rest - part.astype(F32)
        term = lax.dot_general(part, pick, (dims, ((), ())), preferred_element_type=F32)
        total = term if total is None else total + term
    return total


def dot(a, b):
    return lax.dot_general(
        a, b, (((1,), (0,)), ((), ())), precision=lax.Precision.HIGHEST, preferred_element_type=F32
    )


def kernel(
    gxn,
    gyn,
    src_ref,
    coef_ref,
    depth_ref,
    alongx_ref,
    padx_ref,
    first_ref,
    last_ref,
    wavex_ref,
    wavey_ref,
    wavez_ref,
    pick_ref,
    out_ref,
    WB,
    V,
    VQ,
    VP,
    C,
    G,
    DG,
    T,
    W1,
    D1,
    I1,
    C1,
    B1,
    V1,
    VB,
    T1,
    Z,
    G1,
    G2,
    G3,
    DI,
    S1,
    S2,
    CR,
    Q,
    LT,
    M3,
    l0_s,
    l0_r,
    blk_s,
    blk_r,
    g1_s,
    g1_r,
    g2_s,
    g2_r,
    g3_s,
    g3_r,
    c1_s,
    c1_r,
    c2_s,
    c2_r,
    m_sem,
):
    gx = lax.axis_index("gx")
    gy = lax.axis_index("gy")

    def at(dx, dy):
        return (lax.rem(gx + dx + gxn, gxn), lax.rem(gy + dy + gyn, gyn))

    corners = [(dx, dy) for dx in (1, -1) for dy in (1, -1)]
    around = [(1, 0), (-1, 0), (0, 1), (0, -1)] + corners

    barrier = pltpu.get_barrier_semaphore()
    for dx, dy in corners:
        for far in (1, 2):
            pl.semaphore_signal(barrier, inc=1, device_id=at(far * dx, dy), device_id_type=MESH)

    def greet_x(i, carry):
        pl.semaphore_signal(barrier, inc=1, device_id=(lax.rem(gx + 1 + i, gxn), gy), device_id_type=MESH)
        return carry

    def greet_y(i, carry):
        pl.semaphore_signal(barrier, inc=1, device_id=(gx, lax.rem(gy + 1 + i, gyn)), device_id_type=MESH)
        return carry

    lax.fori_loop(0, gxn - 1, greet_x, 0)
    lax.fori_loop(0, gyn - 1, greet_y, 0)

    table_copy = pltpu.make_async_copy(last_ref.at[gy], LT, m_sem)
    table_copy.start()

    def remote(src, dst, ssem, rsem, dev):
        return pltpu.make_async_remote_copy(
            src_ref=src, dst_ref=dst, send_sem=ssem, recv_sem=rsem, device_id=dev, device_id_type=MESH
        )

    def start(copies):
        for copy in copies:
            copy.start()

    def wait(copies):
        for copy in copies:
            copy.wait()

    own = pl.ds(16, 2 * LY)
    wide = pl.ds(8, 48)
    upper, lower = pl.ds(40, 8), pl.ds(16, 8)
    slots = iter(range(64))

    def to(src, dst, where):
        k = next(slots)
        return remote(src, dst, l0_s.at[k], l0_r.at[k], at(*where))

    def ghosts(src, dst, lead, dst_lead, depth):
        x_ends = ((1, LX + 4 - depth, 4 - depth), (-1, 4, LX + 4))
        y_ends = ((1, upper, pl.ds(8, 8)), (-1, lower, pl.ds(48, 8)))
        along_x = [
            to(src.at[lead, pl.ds(a, depth), own], dst.at[dst_lead, pl.ds(b, depth), own], (d, 0)) for d, a, b in x_ends
        ]
        along_y = [
            to(src.at[lead, pl.ds(4, LX), a], dst.at[dst_lead, pl.ds(4, LX), b], (0, d)) for d, a, b in y_ends
        ]
        both = []
        for d, a, _ in x_ends:
            a = LX + 3 if d == 1 else 4
            b = 3 if d == 1 else LX + 4
            for e, p, q in y_ends:
                both.append(to(src.at[lead, pl.ds(a, 1), p], dst.at[dst_lead, pl.ds(b, 1), q], (d, e)))
        return along_x, along_y, both

    def gather(ref, along_gx, ssem, rsem):
        me, count = (gx, gxn) if along_gx else (gy, gyn)

        def peer(i):
            return lax.rem(me + 1 + i, count)

        def send(i, carry):
            dev = (peer(i), gy) if along_gx else (gx, peer(i))
            remote(ref.at[me], ref.at[me], ssem.at[i], rsem.at[me], dev).start()
            return carry

        def finish():
            def take(i, carry):
                dev = (peer(i), gy) if along_gx else (gx, peer(i))
                copy = remote(ref.at[me], ref.at[peer(i)], ssem.at[i], rsem.at[peer(i)], dev)
                copy.wait_send()
                copy.wait_recv()
                return carry

            lax.fori_loop(0, count - 1, take, 0)

        lax.fori_loop(0, count - 1, send, 0)
        return finish

    def iota(shape, dim):
        return lax.broadcasted_iota(jnp.int32, shape, dim)

    def spread(values, x, put):
        even = ((iota((LY, LANES), 0) + x) & 1) == 0
        for h in (0, 1):
            a = values[:, 2 * h * LANES : (2 * h + 1) * LANES]
            b = values[:, (2 * h + 1) * LANES : (2 * h + 2) * LANES]
            put(0, h, jnp.where(even, a, b))
            put(1, h, jnp.where(even, b, a))

    def fill(mixed, plane):
        for x in range(LX):

            def put(c, h, values, x=x):
                WB[plane + c, x + 4, pl.ds(16 + h, LY, stride=2), :] = values

            spread(mixed[x * LY : (x + 1) * LY], x, put)

    for d in range(3):
        flat = coef_ref[d].reshape(LX * LY, 4 * LANES)
        fill(lax.dot_general(flat, pick_ref[...], (((1,), (0,)), ((), ())), preferred_element_type=F32), 2 * d)

    fill(permuted(src_ref[...].reshape(LX * LY, 4 * LANES), pick_ref[...], ((1,), (0,))), 6)
    pl.semaphore_wait(barrier, gxn - 1 + gyn - 1 + 8)

    eight = pl.ds(0, 8)
    wx, wy, wc = ghosts(WB, WB, eight, eight, 1)
    wx.append(to(WB.at[pl.ds(0, 2), LX + 2, own], WB.at[pl.ds(0, 2), 2, own], (1, 0)))
    for e, p, q in ((1, upper, pl.ds(8, 8)), (-1, lower, pl.ds(48, 8))):
        wc.append(to(WB.at[pl.ds(0, 2), LX + 2, p], WB.at[pl.ds(0, 2), 2, q], (1, e)))
    start(wy)
    start(wx)
    start(wc)

    s32 = iota((2 * LY, LANES), 0)
    s48 = iota((48, LANES), 0)
    j8 = iota((8, LANES), 0)
    j12 = iota((12, LANES), 0)
    mine = pl.ds(16, 8)

    def pairs(i, values):
        T[i, pl.ds(0, 32)] = values
        return [T[i, pl.ds(h, 8, stride=4), :] + T[i, pl.ds(h + 2, 8, stride=4), :] for h in (0, 1)]

    def colours(i, two, scale):
        even = ((j8 + i) & 1) == 0
        return jnp.where(even, two[0], two[1]) * scale, jnp.where(even, two[1], two[0]) * scale

    def coarsen(i, carry):
        lo, hi = 4 + 2 * i, 5 + 2 * i
        e, o = colours(i, pairs(i, WB[0, hi, own] + WB[1, hi, own]), 0.0625)
        W1[0, 6 + i, mine] = e
        W1[1, 6 + i, mine] = o
        T[i, pl.ds(0, 32)] = WB[2, lo, own] + WB[3, lo, own] + WB[2, hi, own] + WB[3, hi, own]
        e, o = colours(i, [T[i, pl.ds(2 + h, 8, stride=4), :] for h in (0, 1)], 0.0625)
        W1[2, 6 + i, mine] = e
        W1[3, 6 + i, mine] = o
        even = ((s32 >> 1) & 1) == 0
        low = jnp.where(even, WB[5, lo, own], WB[4, lo, own])
        e, o = colours(i, pairs(i, low + jnp.where(even, WB[4, hi, own], WB[5, hi, own])), 0.0625)
        W1[4, 6 + i, mine] = e
        W1[5, 6 + i, mine] = o
        return carry

    lax.fori_loop(0, 4, coarsen, 0)

    def blocks(src, dst, lead, k):
        near = []
        for i, (dx, dy) in enumerate(around):
            there = dst.at[lead, pl.ds(6 - 4 * dx, 4), pl.ds(16 - 8 * dy, 8)]
            near.append(remote(src.at[lead, pl.ds(6, 4), mine], there, blk_s.at[k, i], blk_r.at[k, i], at(dx, dy)))
        return near

    def second(src, dst, lead, k, sides):
        copies = []
        for dx, a, b in sides:
            for dy in (-1, 0, 1):
                i = 8 + len(copies)
                there = dst.at[lead, pl.ds(b, 1), pl.ds(16 - 8 * dy, 8)]
                copies.append(
                    remote(src.at[lead, pl.ds(a, 1), mine], there, blk_s.at[k, i], blk_r.at[k, i], at(dx, dy))
                )
        return copies

    six, both = pl.ds(0, 6), pl.ds(0, 2)
    w1_copies = blocks(W1, W1, six, 0) + second(W1, W1, pl.ds(0, 2), 0, ((2, 9, 1),))

    sums = [W1[0, 7, mine] + W1[1, 7, mine] + W1[0, 9, mine] + W1[1, 9, mine]]
    part_y, part_z = 0.0, 0.0
    for i in range(4):
        part_y = part_y + jnp.where((j8 & 1) == 1, W1[2, 6 + i, mine] + W1[3, 6 + i, mine], 0.0)
        part_z = part_z + jnp.where(((j8 + i) & 1) == 0, W1[5, 6 + i, mine], W1[4, 6 + i, mine])
    sums += [part_y, part_z]
    scale = 1.0 / (16.0 * 2 * gxn * 4 * gyn * LANES)
    lane = iota((1, LANES), 1)
    row = jnp.zeros((1, LANES), F32)
    for d in range(3):
        value = jnp.sum(jnp.sum(sums[d], axis=0, keepdims=True), axis=1, keepdims=True)
        row = row + jnp.where(lane == d, value * scale, 0.0)
    S1[gy] = row

    def other(read, count, pc0):
        h_zero = (iota((count, LANES), 0) & 1) == 0
        up, down = read(1), read(-1)
        return jnp.where(
            h_zero,
            jnp.where(pc0, pltpu.roll(up, 1, 1), up),
            jnp.where(pc0, down, pltpu.roll(down, LANES - 1, 1)),
        )

    def coefficients(x, carry):
        for c in (0, 1):
            o = 1 - c
            pc0 = (((s48 >> 1) + x + c) & 1) == 0
            xp, xm = WB[c, x, wide], WB[o, x - 1, wide]
            yp, ym = WB[2 + c, x, wide], WB[2 + o, x, pl.ds(6, 48)]
            zc, zo = WB[4 + c, x, wide], WB[4 + o, x, wide]
            zs = jnp.where(pc0, zc, zo)
            far = other(lambda ds: WB[4 + o, x, pl.ds(8 + ds, 48)], 48, pc0)
            zt = jnp.where(pc0, far, zc)
            diagonal = MASS + xp + xm + yp + ym + zs + zt
            inverse = 1.0 / diagonal
            for k, value in enumerate((xp, xm, yp, ym, zs, zt)):
                C[c, k, x] = value * inverse
            DG[c, x] = diagonal
            g = WB[6 + c, x, wide] * inverse
            G[c, x] = g
            if c == 0:
                V[0, x, wide] = g
        return carry

    def weighted(A, c, x, base, count):
        o = 1 - c
        at_base, here = pl.ds(base - 8, count), pl.ds(base, count)
        pc0 = (((iota((count, LANES), 0) >> 1) + x + c) & 1) == 0
        total = G[c, x, at_base] + C[c, 0, x, at_base] * A[o, x + 1, here] + C[c, 1, x, at_base] * A[o, x - 1, here]
        total = total + C[c, 2, x, at_base] * A[o, x, pl.ds(base + 2, count)]
        total = total + C[c, 3, x, at_base] * A[o, x, pl.ds(base - 2, count)]
        far = other(lambda ds: A[o, x, pl.ds(base + ds, count)], count, pc0)
        return total + C[c, 4, x, at_base] * A[o, x, here] + C[c, 5, x, at_base] * far

    def half_sweep(A, c, into, beyond):
        low, base, count = (3, 8, 48) if beyond else (4, 16, 32)

        def rows(i, carry):
            x = low + i
            into[c, x, pl.ds(base, count)] = weighted(A, c, x, base, count)
            return carry

        lax.fori_loop(0, 16 - 2 * low, rows, 0)

    wait(wy)
    lax.fori_loop(0, 2, lambda i, carry: coefficients(5 + 5 * i, carry), 0)
    ends = [
        to(V.at[0, 10, own], V.at[0, 2, own], (1, 0)),
        to(V.at[0, 5, own], V.at[0, 13, own], (-1, 0)),
    ]
    start(ends)
    lax.fori_loop(6, 10, coefficients, 0)
    lax.fori_loop(11, 12, coefficients, 0)
    wait(wx)
    wait(wc)
    lax.fori_loop(3, 5, coefficients, 0)
    lax.fori_loop(12, 13, coefficients, 0)
    wait(ends)
    half_sweep(V, 1, V, True)
    half_sweep(V, 0, VQ, False)
    ex, ey, ec = ghosts(VQ, VQ, 0, 0, 2)
    start(ex)
    start(ey)
    start(ec)
    start(w1_copies)
    wait_c1 = gather(S1, False, c1_s, c1_r)
    wait(ex)
    wait(ey)
    wait(ec)
    half_sweep(VQ, 1, VQ, True)

    def restrict(i, carry):
        total = None
        for parity in (0, 1):
            x = 4 + 2 * i + parity
            for c in (0, 1):
                r = DG[c, x, pl.ds(8, 32)] * (weighted(VQ, c, x, 16, 32) - VQ[c, x, own])
                total = r if total is None else total + r
        e, o = colours(i, pairs(i, total), 0.125)
        B1[0, 6 + i, mine] = e
        B1[1, 6 + i, mine] = o
        return carry

    lax.fori_loop(0, 4, restrict, 0)
    b1_copies = blocks(B1, B1, both, 1)
    start(b1_copies)

    wait_c1()
    S2[gx] = jnp.sum(S1[...], axis=0)
    wait_c2 = gather(S2, True, c2_s, c2_r)

    wait(w1_copies)
    near1 = pl.ds(8, 24)
    s24 = iota((24, LANES), 0)

    def coefficients1(x, carry):
        for c in (0, 1):
            o = 1 - c
            pc0 = ((s24 + x + c) & 1) == 0
            zc, zo = W1[4 + c, x, near1], W1[4 + o, x, near1]
            zs, zt = jnp.where(pc0, zc, zo), jnp.where(pc0, pltpu.roll(zo, 1, 1), zc)
            values = (W1[c, x, near1], W1[o, x - 1, near1], W1[2 + c, x, near1], W1[2 + o, x, pl.ds(7, 24)], zs, zt)
            diagonal = MASS
            for value in values:
                diagonal = diagonal + value
            inverse = 1.0 / diagonal
            D1[c, x] = diagonal
            I1[c, x] = inverse
            for k, value in enumerate(values):
                C1[c, k, x] = value * inverse
        return carry

    lax.fori_loop(2, 14, coefficients1, 0)

    def weighted1(A, c, x):
        o = 1 - c
        pc0 = ((s24 + x + c) & 1) == 0
        here = A[o, x, near1]
        total = B1[c, x, near1] * I1[c, x] + C1[c, 0, x] * A[o, x + 1, near1] + C1[c, 1, x] * A[o, x - 1, near1]
        total = total + C1[c, 2, x] * A[o, x, pl.ds(9, 24)] + C1[c, 3, x] * A[o, x, pl.ds(7, 24)]
        far = jnp.where(pc0, pltpu.roll(here, 1, 1), pltpu.roll(here, LANES - 1, 1))
        return total + C1[c, 4, x] * here + C1[c, 5, x] * far

    def half_sweep1(A, c, low):
        def rows(i, carry):
            x = low + i
            A[c, x, near1] = weighted1(A, c, x)
            return carry

        lax.fori_loop(0, 16 - 2 * low, rows, 0)

    wait(b1_copies)

    def first1(x, carry):
        V1[0, x, near1] = B1[0, x, near1] * I1[0, x]
        return carry

    lax.fori_loop(2, 14, first1, 0)
    half_sweep1(V1, 1, 3)
    half_sweep1(V1, 0, 4)
    half_sweep1(V1, 1, 5)

    for i in range(2):
        total = None
        for k in range(2):
            x = 6 + 2 * i + k
            for c in (0, 1):
                r = ((weighted1(V1, c, x) - V1[c, x, near1]) * D1[c, x])[8:16]
                total = r if total is None else total + r
        T1[pl.ds(8, 8), :] = total
        Z[pl.ds(4 * i, 4), :] = (T1[pl.ds(8, 4, stride=2), :] + T1[pl.ds(9, 4, stride=2), :]) * 0.125

    G1[gy] = dot(Z[...], depth_ref[...])
    finish = gather(G1, False, g1_s, g1_r)
    one = pl.ds(1, 1)
    v1_copies = blocks(V1, VB, one, 2) + second(V1, VB, one, 2, ((2, 9, 1), (-2, 6, 14)))
    start(v1_copies)
    vx, vy, vc = ghosts(VQ, VP, 1, 1, 2)
    start(vy)

    wait_c2()
    CR[...] = jnp.sum(S2[...], axis=0)
    mean = [jnp.sum(jnp.where(lane == d, CR[...], 0.0), axis=1, keepdims=True) for d in range(3)]
    cells = float(2 * gxn * 4 * gyn * LANES)
    flat_part = MASS + mean[1] * wavey_ref[gy] + mean[2] * wavez_ref[...]

    def eigen(i, carry):
        tile = pl.ds(pl.multiple_of(8 * i, 8), 8)
        DI[tile, :] = 1.0 / ((flat_part + mean[0] * wavex_ref[tile, :]) * cells)
        return carry

    lax.fori_loop(0, gxn, eigen, 0)
    VB[1, pl.ds(6, 4), mine] = V1[1, pl.ds(6, 4), mine]
    VP[1, pl.ds(4, LX), own] = VQ[1, pl.ds(4, LX), own]
    finish()
    G2[gx] = dot(first_ref[gy], G1[...].reshape(8 * gyn, LANES))
    finish = gather(G2, True, g2_s, g2_r)
    start(vx)
    start(vc)
    table_copy.wait()
    column_x = (iota((16, 32 * gyn), 1) >> 2) & 7
    for x in range(8):
        M3[pl.ds(16 * x, 16), :] = jnp.where(column_x == x, LT[...], 0.0)
    finish()
    spectrum = dot(alongx_ref[...], G2[...].reshape(8 * gxn, LANES)) * DI[...]
    back_x = dot(padx_ref[pl.ds(pl.multiple_of(8 * gx, 8), 32), :], spectrum)
    G3[gy] = dot(back_x, depth_ref[...])
    finish = gather(G3, False, g3_s, g3_r)
    wait(v1_copies)
    wait(vy)
    wait(vx)
    wait(vc)
    finish()
    coarse = dot(M3[...], G3[...].reshape(32 * gyn, LANES))

    for a in range(8):
        part = coarse[16 * a : 16 * a + 16]
        T1[pl.ds(2, 16, stride=2), :] = part
        T1[pl.ds(3, 16, stride=2), :] = part
        for x in (2 * a, 2 * a + 1):
            VB[1, x, near1] = VB[1, x, near1] + T1[pl.ds(0, 24), :]
    half_sweep1(VB, 0, 2)
    half_sweep1(VB, 1, 3)
    half_sweep1(VB, 0, 4)
    half_sweep1(VB, 1, 5)

    def prolong(i, carry):
        even = ((j12 + i) & 1) == 0
        e, o = VB[0, 4 + i, pl.ds(14, 12)], VB[1, 4 + i, pl.ds(14, 12)]
        for h, part in enumerate((jnp.where(even, e, o), jnp.where(even, o, e))):
            T[i, pl.ds(h, 12, stride=4), :] = part
            T[i, pl.ds(h + 2, 12, stride=4), :] = part
        for x in (2 * i, 2 * i + 1):
            VP[1, x, wide] = VP[1, x, wide] + T[i]
        return carry

    lax.fori_loop(1, 7, prolong, 0)
    half_sweep(VP, 0, VP, True)
    half_sweep(VP, 1, V, False)
    ex, ey, ec = ghosts(V, V, 1, 1, 2)
    start(ex)
    start(ey)
    start(ec)
    wait(ex)
    wait(ey)
    wait(ec)
    half_sweep(V, 0, V, True)
    half_sweep(V, 1, V, False)

    for x in range(LX):
        even = ((iota((LY, LANES), 0) + x) & 1) == 0
        for h in (0, 1):
            e, o = V[0, x + 4, pl.ds(16 + h, LY, stride=2), :], V[1, x + 4, pl.ds(16 + h, LY, stride=2), :]
            rows = pl.ds(x * LY, LY)
            Q[rows, pl.ds(2 * h * LANES, LANES)] = jnp.where(even, e, o)
            Q[rows, pl.ds((2 * h + 1) * LANES, LANES)] = jnp.where(even, o, e)
    out_ref[...] = permuted(Q[...], pick_ref[...], ((1,), (1,))).reshape(LX, LY, 4 * LANES)


def solution(mesh):
    gxn, gyn = mesh.shape["gx"], mesh.shape["gy"]
    consts = tables(gxn, gyn)

    def step(source, face_coef):
        vmem = pl.BlockSpec(memory_space=pltpu.VMEM)
        dma = pltpu.SemaphoreType.DMA
        V = pltpu.VMEM
        return pl.pallas_call(
            functools.partial(kernel, gxn, gyn),
            out_shape=jax.ShapeDtypeStruct((LX, LY, 4 * LANES), F32),
            in_specs=[vmem] * 6 + [pl.BlockSpec(memory_space=pl.ANY)] + [vmem] * 4,
            out_specs=vmem,
            scratch_shapes=[
                V((8, 16, 64, LANES), F32),
                V((2, 16, 64, LANES), F32),
                V((2, 16, 64, LANES), F32),
                V((2, 16, 64, LANES), F32),
                V((2, 6, 16, 48, LANES), F32),
                V((2, 16, 48, LANES), F32),
                V((2, 16, 48, LANES), F32),
                V((8, 48, LANES), F32),
                V((6, 16, 40, LANES), F32),
                V((2, 16, 24, LANES), F32),
                V((2, 16, 24, LANES), F32),
                V((2, 6, 16, 24, LANES), F32),
                V((2, 16, 40, LANES), F32),
                V((2, 16, 40, LANES), F32),
                V((2, 16, 40, LANES), F32),
                V((40, LANES), F32),
                V((8, LANES), F32),
                V((gyn, 8, LANES), F32),
                V((gxn, 8, LANES), F32),
                V((gyn, 32, LANES), F32),
                V((8 * gxn, LANES), F32),
                V((gyn, 1, LANES), F32),
                V((gxn, 1, LANES), F32),
                V((1, LANES), F32),
                V((LX * LY, 4 * LANES), F32),
                V((16, 32 * gyn), F32),
                V((128, 32 * gyn), F32),
                dma((48,)),
                dma((48,)),
                dma((3, 14)),
                dma((3, 14)),
                dma((gyn,)),
                dma((gyn,)),
                dma((gxn,)),
                dma((gxn,)),
                dma((gyn,)),
                dma((gyn,)),
                dma((gyn,)),
                dma((gyn,)),
                dma((gxn,)),
                dma((gxn,)),
                dma,
            ],
            compiler_params=pltpu.CompilerParams(
                collective_id=0, has_side_effects=True, vmem_limit_bytes=60 * 1024 * 1024
            ),
            name="cycle",
        )(source, face_coef, *[jnp.asarray(t) for t in consts])

    return jax.shard_map(
        step,
        mesh=mesh,
        in_specs=(P("gx", "gy", None), P(None, "gx", "gy", None)),
        out_specs=P("gx", "gy", None),
        check_vma=False,
    )
```

time: 95.6 us -> 83.5 us (0.87)
  Pallas kernels: 93.7 us -> 81.6 us
    pallas_call x1, Pallas kernels: 93.7 us -> 81.6 us  [step(): pl.pallas_call(functools.partial(kernel, gxn, gyn), out_shape=jax.ShapeDt...]
where the time goes in v2:
time: 83.5 us; the launch traced here: 83.3 us
  Pallas kernels  81.6 us (98%)
  local copies, waits for them, and re-layouts  1.67 us (2%)
    pallas_call x1, Pallas kernels, step(): pl.pallas_call(functools.partial(kernel, gxn, gyn), out_shape=jax.ShapeDt...  81.6 us
    unnamed x1, local copies, waits for them, and re-layouts  1.67 us

profile of v2, /device:TPU:1, one launch (start us, length us, event | category | flops | bytes accessed | tf_op | source)
XLA Modules:
  0.0 83.3 jit_solution(13660760534118954013)
XLA Ops:
  0.0 81.6 %cycle.1 = f32[8,16,512]{2,1,0:T(8,128)} custom-call(f32[8,16,512]{2,1,0:T(8,128)} %src_ref.1, bf16[3,8,16,512]{3,2,1,0:T(8,128)(2,1)} %coef_ref.1, f32[128,128]{1,0:T(8,128)} %constant.18.clone.depth_ref, f32[256,256]{1,0:T(8,128)} %constant.19.clone.alongx_ref, f32[280,256]{1,0:T(8,128)} %constant.20.clone.padx_ref, ...), custom_call_target="tpu_custom_call" | custom-call | tf_op jit(solution)/shard_map/cycle/pallas_call | solution.py:574
  81.6 1.7 %copy.13 = f32[8,16,512]{2,1,0:T(8,128)} copy(f32[8,16,512]{2,1,0:T(8,128)} %cycle.1) | data formatting | bytes 524288

commit v3 on v2

--- a/solution.py
+++ b/solution.py
@@ -46,7 +46,9 @@
     pick = np.zeros((4 * LANES, 4 * LANES))
     column = np.arange(4 * LANES)
     pick[4 * (column % LANES) + column // LANES, column] = 1.0
-    out = [np.asarray(t, np.float32) for t in (depth, along_x, padded, first, last, wave_x, wave_y, wave_z)]
+    stacked = np.concatenate([depth, wave_x, wave_z])
+    both_x = np.concatenate([along_x, padded])
+    out = [np.asarray(t, np.float32) for t in (stacked, both_x, first, last, wave_y)]
     return out + [pick.astype(jnp.bfloat16)]
 
 
@@ -72,14 +74,11 @@
     gyn,
     src_ref,
     coef_ref,
-    depth_ref,
-    alongx_ref,
-    padx_ref,
-    first_ref,
-    last_ref,
-    wavex_ref,
-    wavey_ref,
-    wavez_ref,
+    stacked_hbm,
+    alongx_hbm,
+    first_hbm,
+    last_hbm,
+    wavey_hbm,
     pick_ref,
     out_ref,
     WB,
@@ -109,21 +108,15 @@
     Q,
     LT,
     M3,
-    l0_s,
-    l0_r,
-    blk_s,
-    blk_r,
-    g1_s,
-    g1_r,
-    g2_s,
-    g2_r,
-    g3_s,
-    g3_r,
-    c1_s,
-    c1_r,
-    c2_s,
-    c2_r,
-    m_sem,
+    GE,
+    STK,
+    AX,
+    FI,
+    WY,
+    SPARE,
+    group_s,
+    group_r,
+    local,
 ):
     gx = lax.axis_index("gx")
     gy = lax.axis_index("gy")
@@ -150,68 +143,73 @@
     lax.fori_loop(0, gxn - 1, greet_x, 0)
     lax.fori_loop(0, gyn - 1, greet_y, 0)
 
-    table_copy = pltpu.make_async_copy(last_ref.at[gy], LT, m_sem)
-    table_copy.start()
+    table_copies = [
+        pltpu.make_async_copy(a, b, local.at[i])
+        for i, (a, b) in enumerate(
+            ((last_hbm.at[gy], LT), (stacked_hbm, STK), (alongx_hbm, AX), (first_hbm.at[gy], FI), (wavey_hbm.at[gy], WY))
+        )
+    ]
+    for copy in table_copies:
+        copy.start()
 
     def remote(src, dst, ssem, rsem, dev):
         return pltpu.make_async_remote_copy(
             src_ref=src, dst_ref=dst, send_sem=ssem, recv_sem=rsem, device_id=dev, device_id_type=MESH
         )
 
-    def start(copies):
-        for copy in copies:
-            copy.start()
-
-    def wait(copies):
-        for copy in copies:
-            copy.wait()
+    groups = iter(range(32))
+
+    class Group:
+        def __init__(self):
+            k = next(groups)
+            self.send, self.recv, self.rows = group_s.at[k], group_r.at[k], 0
+
+        def start(self, copies):
+            for src, dst, where in copies:
+                self.rows += int(np.prod(src.shape)) // LANES
+                remote(src, dst, self.send, self.recv, at(*where)).start()
+
+        def wait(self):
+            whole = SPARE.at[pl.ds(0, self.rows)]
+            copy = remote(whole, whole, self.send, self.recv, at(1, 0))
+            copy.wait_send()
+            copy.wait_recv()
 
     own = pl.ds(16, 2 * LY)
     wide = pl.ds(8, 48)
     upper, lower = pl.ds(40, 8), pl.ds(16, 8)
-    slots = iter(range(64))
-
-    def to(src, dst, where):
-        k = next(slots)
-        return remote(src, dst, l0_s.at[k], l0_r.at[k], at(*where))
-
     def ghosts(src, dst, lead, dst_lead, depth):
         x_ends = ((1, LX + 4 - depth, 4 - depth), (-1, 4, LX + 4))
         y_ends = ((1, upper, pl.ds(8, 8)), (-1, lower, pl.ds(48, 8)))
         along_x = [
-            to(src.at[lead, pl.ds(a, depth), own], dst.at[dst_lead, pl.ds(b, depth), own], (d, 0)) for d, a, b in x_ends
+            (src.at[lead, pl.ds(a, depth), own], dst.at[dst_lead, pl.ds(b, depth), own], (d, 0)) for d, a, b in x_ends
         ]
         along_y = [
-            to(src.at[lead, pl.ds(4, LX), a], dst.at[dst_lead, pl.ds(4, LX), b], (0, d)) for d, a, b in y_ends
+            (src.at[lead, pl.ds(4, LX), a], dst.at[dst_lead, pl.ds(4, LX), b], (0, d)) for d, a, b in y_ends
         ]
         both = []
         for d, a, _ in x_ends:
             a = LX + 3 if d == 1 else 4
             b = 3 if d == 1 else LX + 4
             for e, p, q in y_ends:
-                both.append(to(src.at[lead, pl.ds(a, 1), p], dst.at[dst_lead, pl.ds(b, 1), q], (d, e)))
+                both.append((src.at[lead, pl.ds(a, 1), p], dst.at[dst_lead, pl.ds(b, 1), q], (d, e)))
         return along_x, along_y, both
 
-    def gather(ref, along_gx, ssem, rsem):
+    def gather(ref, along_gx):
         me, count = (gx, gxn) if along_gx else (gy, gyn)
-
-        def peer(i):
-            return lax.rem(me + 1 + i, count)
+        k = next(groups)
 
         def send(i, carry):
-            dev = (peer(i), gy) if along_gx else (gx, peer(i))
-            remote(ref.at[me], ref.at[me], ssem.at[i], rsem.at[me], dev).start()
+            peer = lax.rem(me + 1 + i, count)
+            dev = (peer, gy) if along_gx else (gx, peer)
+            remote(ref.at[me], ref.at[me], group_s.at[k], group_r.at[k], dev).start()
             return carry
 
         def finish():
-            def take(i, carry):
-                dev = (peer(i), gy) if along_gx else (gx, peer(i))
-                copy = remote(ref.at[me], ref.at[peer(i)], ssem.at[i], rsem.at[peer(i)], dev)
-                copy.wait_send()
-                copy.wait_recv()
-                return carry
-
-            lax.fori_loop(0, count - 1, take, 0)
+            whole = ref.at[pl.ds(0, count - 1)]
+            copy = remote(whole, whole, group_s.at[k], group_r.at[k], at(1, 0))
+            copy.wait_send()
+            copy.wait_recv()
 
         lax.fori_loop(0, count - 1, send, 0)
         return finish
@@ -242,14 +240,19 @@
     fill(permuted(src_ref[...].reshape(LX * LY, 4 * LANES), pick_ref[...], ((1,), (0,))), 6)
     pl.semaphore_wait(barrier, gxn - 1 + gyn - 1 + 8)
 
-    eight = pl.ds(0, 8)
+    first_y, rest_y, all_x = Group(), Group(), Group()
+    low_high = (upper, pl.ds(8, 8)), (lower, pl.ds(48, 8))
+    inner = pl.ds(4, LX)
+    first_y.start([(WB.at[pl.ds(2, 2), inner, upper], WB.at[pl.ds(2, 2), inner, pl.ds(8, 8)], (0, 1))])
+    eight, pair = pl.ds(0, 8), pl.ds(0, 2)
     wx, wy, wc = ghosts(WB, WB, eight, eight, 1)
-    wx.append(to(WB.at[pl.ds(0, 2), LX + 2, own], WB.at[pl.ds(0, 2), 2, own], (1, 0)))
-    for e, p, q in ((1, upper, pl.ds(8, 8)), (-1, lower, pl.ds(48, 8))):
-        wc.append(to(WB.at[pl.ds(0, 2), LX + 2, p], WB.at[pl.ds(0, 2), 2, q], (1, e)))
-    start(wy)
-    start(wx)
-    start(wc)
+    all_x.start(wx)
+    all_x.start([(WB.at[pair, LX + 2, own], WB.at[pair, 2, own], (1, 0))])
+    rest_y.start(
+        [(WB.at[p, inner, upper], WB.at[p, inner, pl.ds(8, 8)], (0, 1)) for p in (pair, pl.ds(4, 4))] + wy[1:]
+    )
+    all_x.start(wc)
+    all_x.start([(WB.at[pair, LX + 2, p], WB.at[pair, 2, q], (1, e)) for e, (p, q) in zip((1, -1), low_high)])
 
     s32 = iota((2 * LY, LANES), 0)
     s48 = iota((48, LANES), 0)
@@ -283,26 +286,20 @@
 
     lax.fori_loop(0, 4, coarsen, 0)
 
-    def blocks(src, dst, lead, k):
-        near = []
-        for i, (dx, dy) in enumerate(around):
-            there = dst.at[lead, pl.ds(6 - 4 * dx, 4), pl.ds(16 - 8 * dy, 8)]
-            near.append(remote(src.at[lead, pl.ds(6, 4), mine], there, blk_s.at[k, i], blk_r.at[k, i], at(dx, dy)))
-        return near
-
-    def second(src, dst, lead, k, sides):
-        copies = []
-        for dx, a, b in sides:
-            for dy in (-1, 0, 1):
-                i = 8 + len(copies)
-                there = dst.at[lead, pl.ds(b, 1), pl.ds(16 - 8 * dy, 8)]
-                copies.append(
-                    remote(src.at[lead, pl.ds(a, 1), mine], there, blk_s.at[k, i], blk_r.at[k, i], at(dx, dy))
-                )
-        return copies
+    def blocks(src, dst, lead):
+        return [
+            (src.at[lead, pl.ds(6, 4), mine], dst.at[lead, pl.ds(6 - 4 * dx, 4), pl.ds(16 - 8 * dy, 8)], (dx, dy))
+            for dx, dy in around
+        ]
+
+    def second(src, dst, lead, sides):
+        return [
+            (src.at[lead, pl.ds(a, 1), mine], dst.at[lead, pl.ds(b, 1), pl.ds(16 - 8 * dy, 8)], (dx, dy))
+            for dx, a, b in sides
+            for dy in (-1, 0, 1)
+        ]
 
     six, both = pl.ds(0, 6), pl.ds(0, 2)
-    w1_copies = blocks(W1, W1, six, 0) + second(W1, W1, pl.ds(0, 2), 0, ((2, 9, 1),))
 
     sums = [W1[0, 7, mine] + W1[1, 7, mine] + W1[0, 9, mine] + W1[1, 9, mine]]
     part_y, part_z = 0.0, 0.0
@@ -358,41 +355,55 @@
         far = other(lambda ds: A[o, x, pl.ds(base + ds, count)], count, pc0)
         return total + C[c, 4, x, at_base] * A[o, x, here] + C[c, 5, x, at_base] * far
 
-    def half_sweep(A, c, into, beyond):
-        low, base, count = (3, 8, 48) if beyond else (4, 16, 32)
-
-        def rows(i, carry):
-            x = low + i
+    def update(A, c, into, low, high, base=16, count=32):
+        def rows(x, carry):
             into[c, x, pl.ds(base, count)] = weighted(A, c, x, base, count)
             return carry
 
-        lax.fori_loop(0, 16 - 2 * low, rows, 0)
-
-    wait(wy)
-    lax.fori_loop(0, 2, lambda i, carry: coefficients(5 + 5 * i, carry), 0)
-    ends = [
-        to(V.at[0, 10, own], V.at[0, 2, own], (1, 0)),
-        to(V.at[0, 5, own], V.at[0, 13, own], (-1, 0)),
-    ]
-    start(ends)
-    lax.fori_loop(6, 10, coefficients, 0)
-    lax.fori_loop(11, 12, coefficients, 0)
-    wait(wx)
-    wait(wc)
+        lax.fori_loop(low, high, rows, 0)
+
+    def half_sweep(A, c, into, beyond):
+        if beyond:
+            update(A, c, into, 3, 13, 8, 48)
+        else:
+            update(A, c, into, 4, 12)
+
+    def ends(i, carry):
+        x = 5 + 5 * i
+        pc0 = (((s32 >> 1) + x) & 1) == 0
+        diagonal = MASS + WB[0, x, own] + WB[1, x - 1, own] + WB[2, x, own] + WB[3, x, pl.ds(14, 32)]
+        far = WB[5, x, own]
+        far = other(lambda ds: pltpu.roll(far, (2 * LY - ds) % (2 * LY), 0), 32, pc0)
+        diagonal = diagonal + jnp.where(pc0, WB[4, x, own], WB[5, x, own]) + jnp.where(pc0, far, WB[4, x, own])
+        GE[i] = WB[6, x, own] / diagonal
+        return carry
+
+    first_y.wait()
+    lax.fori_loop(0, 2, ends, 0)
+    outer = Group()
+    outer.start([(GE.at[1], V.at[0, 2, own], (1, 0)), (GE.at[0], V.at[0, 13, own], (-1, 0))])
+    w1_group = Group()
+    w1_group.start(blocks(W1, W1, six) + second(W1, W1, pair, ((2, 9, 1),)))
+    wait_c1 = gather(S1, False)
+    rest_y.wait()
+    lax.fori_loop(5, 12, coefficients, 0)
+    all_x.wait()
     lax.fori_loop(3, 5, coefficients, 0)
     lax.fori_loop(12, 13, coefficients, 0)
-    wait(ends)
+    outer.wait()
     half_sweep(V, 1, V, True)
-    half_sweep(V, 0, VQ, False)
-    ex, ey, ec = ghosts(VQ, VQ, 0, 0, 2)
-    start(ex)
-    start(ey)
-    start(ec)
-    start(w1_copies)
-    wait_c1 = gather(S1, False, c1_s, c1_r)
-    wait(ex)
-    wait(ey)
-    wait(ec)
+
+    def exchanged(A, c, into):
+        layers = Group()
+        ex, ey, ec = ghosts(into, into, c, c, 2)
+        update(A, c, into, 4, 6)
+        update(A, c, into, 10, 12)
+        layers.start(ex + ec)
+        update(A, c, into, 6, 10)
+        layers.start(ey)
+        layers.wait()
+
+    exchanged(V, 0, VQ)
     half_sweep(VQ, 1, VQ, True)
 
     def restrict(i, carry):
@@ -408,14 +419,14 @@
         return carry
 
     lax.fori_loop(0, 4, restrict, 0)
-    b1_copies = blocks(B1, B1, both, 1)
-    start(b1_copies)
+    b1_group = Group()
+    b1_group.start(blocks(B1, B1, both))
 
     wait_c1()
     S2[gx] = jnp.sum(S1[...], axis=0)
-    wait_c2 = gather(S2, True, c2_s, c2_r)
-
-    wait(w1_copies)
+    wait_c2 = gather(S2, True)
+
+    w1_group.wait()
     near1 = pl.ds(8, 24)
     s24 = iota((24, LANES), 0)
 
@@ -455,7 +466,7 @@
 
         lax.fori_loop(0, 16 - 2 * low, rows, 0)
 
-    wait(b1_copies)
+    b1_group.wait()
 
     def first1(x, carry):
         V1[0, x, near1] = B1[0, x, near1] * I1[0, x]
@@ -476,46 +487,46 @@
         T1[pl.ds(8, 8), :] = total
         Z[pl.ds(4 * i, 4), :] = (T1[pl.ds(8, 4, stride=2), :] + T1[pl.ds(9, 4, stride=2), :]) * 0.125
 
-    G1[gy] = dot(Z[...], depth_ref[...])
-    finish = gather(G1, False, g1_s, g1_r)
+    for copy in table_copies:
+        copy.wait()
+    depth = pl.ds(0, LANES)
+    G1[gy] = dot(Z[...], STK[depth, :])
+    finish = gather(G1, False)
     one = pl.ds(1, 1)
-    v1_copies = blocks(V1, VB, one, 2) + second(V1, VB, one, 2, ((2, 9, 1), (-2, 6, 14)))
-    start(v1_copies)
+    v1_group = Group()
+    v1_group.start(blocks(V1, VB, one) + second(V1, VB, one, ((2, 9, 1), (-2, 6, 14))))
+    v_group = Group()
     vx, vy, vc = ghosts(VQ, VP, 1, 1, 2)
-    start(vy)
+    v_group.start(vy)
 
     wait_c2()
     CR[...] = jnp.sum(S2[...], axis=0)
     mean = [jnp.sum(jnp.where(lane == d, CR[...], 0.0), axis=1, keepdims=True) for d in range(3)]
     cells = float(2 * gxn * 4 * gyn * LANES)
-    flat_part = MASS + mean[1] * wavey_ref[gy] + mean[2] * wavez_ref[...]
+    flat_part = MASS + mean[1] * WY[...] + mean[2] * STK[pl.ds(LANES + 8 * gxn, 8), :]
 
     def eigen(i, carry):
         tile = pl.ds(pl.multiple_of(8 * i, 8), 8)
-        DI[tile, :] = 1.0 / ((flat_part + mean[0] * wavex_ref[tile, :]) * cells)
+        DI[tile, :] = 1.0 / ((flat_part + mean[0] * STK[pl.ds(pl.multiple_of(LANES + 8 * i, 8), 8), :]) * cells)
         return carry
 
     lax.fori_loop(0, gxn, eigen, 0)
     VB[1, pl.ds(6, 4), mine] = V1[1, pl.ds(6, 4), mine]
     VP[1, pl.ds(4, LX), own] = VQ[1, pl.ds(4, LX), own]
     finish()
-    G2[gx] = dot(first_ref[gy], G1[...].reshape(8 * gyn, LANES))
-    finish = gather(G2, True, g2_s, g2_r)
-    start(vx)
-    start(vc)
-    table_copy.wait()
+    G2[gx] = dot(FI[...], G1[...].reshape(8 * gyn, LANES))
+    finish = gather(G2, True)
+    v_group.start(vx + vc)
     column_x = (iota((16, 32 * gyn), 1) >> 2) & 7
     for x in range(8):
         M3[pl.ds(16 * x, 16), :] = jnp.where(column_x == x, LT[...], 0.0)
     finish()
-    spectrum = dot(alongx_ref[...], G2[...].reshape(8 * gxn, LANES)) * DI[...]
-    back_x = dot(padx_ref[pl.ds(pl.multiple_of(8 * gx, 8), 32), :], spectrum)
-    G3[gy] = dot(back_x, depth_ref[...])
-    finish = gather(G3, False, g3_s, g3_r)
-    wait(v1_copies)
-    wait(vy)
-    wait(vx)
-    wait(vc)
+    spectrum = dot(AX[pl.ds(0, 8 * gxn), :], G2[...].reshape(8 * gxn, LANES)) * DI[...]
+    back_x = dot(AX[pl.ds(pl.multiple_of(8 * gxn + 8 * gx, 8), 32), :], spectrum)
+    G3[gy] = dot(back_x, STK[depth, :])
+    finish = gather(G3, False)
+    v1_group.wait()
+    v_group.wait()
     finish()
     coarse = dot(M3[...], G3[...].reshape(32 * gyn, LANES))
 
@@ -542,14 +553,7 @@
 
     lax.fori_loop(1, 7, prolong, 0)
     half_sweep(VP, 0, VP, True)
-    half_sweep(VP, 1, V, False)
-    ex, ey, ec = ghosts(V, V, 1, 1, 2)
-    start(ex)
-    start(ey)
-    start(ec)
-    wait(ex)
-    wait(ey)
-    wait(ec)
+    exchanged(VP, 1, V)
     half_sweep(V, 0, V, True)
     half_sweep(V, 1, V, False)
 
@@ -574,7 +578,7 @@
         return pl.pallas_call(
             functools.partial(kernel, gxn, gyn),
             out_shape=jax.ShapeDtypeStruct((LX, LY, 4 * LANES), F32),
-            in_specs=[vmem] * 6 + [pl.BlockSpec(memory_space=pl.ANY)] + [vmem] * 4,
+            in_specs=[vmem] * 2 + [pl.BlockSpec(memory_space=pl.ANY)] * 5 + [vmem],
             out_specs=vmem,
             scratch_shapes=[
                 V((8, 16, 64, LANES), F32),
@@ -604,21 +608,15 @@
                 V((LX * LY, 4 * LANES), F32),
                 V((16, 32 * gyn), F32),
                 V((128, 32 * gyn), F32),
-                dma((48,)),
-                dma((48,)),
-                dma((3, 14)),
-                dma((3, 14)),
-                dma((gyn,)),
-                dma((gyn,)),
-                dma((gxn,)),
-                dma((gxn,)),
-                dma((gyn,)),
-                dma((gyn,)),
-                dma((gyn,)),
-                dma((gyn,)),
-                dma((gxn,)),
-                dma((gxn,)),
-                dma,
+                V((2, 32, LANES), F32),
+                V((LANES + 8 * gxn + 8, LANES), F32),
+                V((16 * gxn + 24, 8 * gxn), F32),
+                V((8, 8 * gyn), F32),
+                V((8, LANES), F32),
+                V((2048, LANES), F32),
+                dma((15,)),
+                dma((15,)),
+                dma((5,)),
             ],
             compiler_params=pltpu.CompilerParams(
                 collective_id=0, has_side_effects=True, vmem_limit_bytes=60 * 1024 * 1024

time: 83.5 us -> 79 us (0.946)
  Pallas kernels: 81.6 us -> 77.2 us
    pallas_call x1, Pallas kernels: 81.6 us -> 77.2 us  [step(): pl.pallas_call(functools.partial(kernel, gxn, gyn), out_shape=jax.ShapeDt...]
where the time goes in v3:
time: 79 us; the launch traced here: 78.8 us
  Pallas kernels  77.2 us (98%)
  local copies, waits for them, and re-layouts  1.67 us (2%)
    pallas_call x1, Pallas kernels, step(): pl.pallas_call(functools.partial(kernel, gxn, gyn), out_shape=jax.ShapeDt...  77.2 us
    unnamed x1, local copies, waits for them, and re-layouts  1.67 us

profile of v3, /device:TPU:1, one launch (start us, length us, event | category | flops | bytes accessed | tf_op | source)
XLA Modules:
  0.0 78.8 jit_solution(14516076042038734384)
XLA Ops:
  0.0 77.2 %cycle.1 = f32[8,16,512]{2,1,0:T(8,128)} custom-call(f32[8,16,512]{2,1,0:T(8,128)} %src_ref.1, bf16[3,8,16,512]{3,2,1,0:T(8,128)(2,1)} %coef_ref.1, f32[392,128]{1,0:T(8,128)} %constant.12.clone.stacked_hbm, f32[536,256]{1,0:T(8,128)} %constant.13.clone.alongx_hbm, f32[16,8,128]{2,1,0:T(8,128)} %constant.14.clone.first_hbm, ...), custom_call_target="tpu_custom_call" | custom-call | tf_op jit(solution)/shard_map/cycle/pallas_call | solution.py:578
  77.2 1.7 %copy.10 = f32[8,16,512]{2,1,0:T(8,128)} copy(f32[8,16,512]{2,1,0:T(8,128)} %cycle.1) | data formatting | bytes 524288

commit v4 on v3

--- a/solution.py
+++ b/solution.py
@@ -191,7 +191,7 @@
         for d, a, _ in x_ends:
             a = LX + 3 if d == 1 else 4
             b = 3 if d == 1 else LX + 4
-            for e, p, q in y_ends:
+            for e, p, q in ((1, pl.ds(44, 4), pl.ds(12, 4)), (-1, pl.ds(16, 4), pl.ds(48, 4))):
                 both.append((src.at[lead, pl.ds(a, 1), p], dst.at[dst_lead, pl.ds(b, 1), q], (d, e)))
         return along_x, along_y, both
 
@@ -241,7 +241,7 @@
     pl.semaphore_wait(barrier, gxn - 1 + gyn - 1 + 8)
 
     first_y, rest_y, all_x = Group(), Group(), Group()
-    low_high = (upper, pl.ds(8, 8)), (lower, pl.ds(48, 8))
+    low_high = (pl.ds(44, 4), pl.ds(12, 4)), (pl.ds(16, 4), pl.ds(48, 4))
     inner = pl.ds(4, LX)
     first_y.start([(WB.at[pl.ds(2, 2), inner, upper], WB.at[pl.ds(2, 2), inner, pl.ds(8, 8)], (0, 1))])
     eight, pair = pl.ds(0, 8), pl.ds(0, 2)
@@ -287,10 +287,14 @@
     lax.fori_loop(0, 4, coarsen, 0)
 
     def blocks(src, dst, lead):
-        return [
-            (src.at[lead, pl.ds(6, 4), mine], dst.at[lead, pl.ds(6 - 4 * dx, 4), pl.ds(16 - 8 * dy, 8)], (dx, dy))
-            for dx, dy in around
-        ]
+        copies = []
+        for dx, dy in around:
+            a, count = 16, 8
+            if dx and dy:
+                a, count = (19, 5) if dy == 1 else (16, 5)
+            there = dst.at[lead, pl.ds(6 - 4 * dx, 4), pl.ds(a - 8 * dy, count)]
+            copies.append((src.at[lead, pl.ds(6, 4), pl.ds(a, count)], there, (dx, dy)))
+        return copies
 
     def second(src, dst, lead, sides):
         return [
@@ -360,7 +364,7 @@
             into[c, x, pl.ds(base, count)] = weighted(A, c, x, base, count)
             return carry
 
-        lax.fori_loop(low, high, rows, 0)
+        lax.fori_loop(low, high, rows, 0, unroll=(high - low) // 2)
 
     def half_sweep(A, c, into, beyond):
         if beyond:
@@ -379,16 +383,15 @@
         return carry
 
     first_y.wait()
-    lax.fori_loop(0, 2, ends, 0)
+    lax.fori_loop(0, 2, ends, 0, unroll=2)
     outer = Group()
     outer.start([(GE.at[1], V.at[0, 2, own], (1, 0)), (GE.at[0], V.at[0, 13, own], (-1, 0))])
     w1_group = Group()
-    w1_group.start(blocks(W1, W1, six) + second(W1, W1, pair, ((2, 9, 1),)))
     wait_c1 = gather(S1, False)
     rest_y.wait()
     lax.fori_loop(5, 12, coefficients, 0)
     all_x.wait()
-    lax.fori_loop(3, 5, coefficients, 0)
+    lax.fori_loop(3, 5, coefficients, 0, unroll=2)
     lax.fori_loop(12, 13, coefficients, 0)
     outer.wait()
     half_sweep(V, 1, V, True)
@@ -401,6 +404,8 @@
         layers.start(ex + ec)
         update(A, c, into, 6, 10)
         layers.start(ey)
+        if into is VQ:
+            w1_group.start(blocks(W1, W1, six) + second(W1, W1, pair, ((2, 9, 1),)))
         layers.wait()
 
     exchanged(V, 0, VQ)
@@ -418,9 +423,12 @@
         B1[1, 6 + i, mine] = o
         return carry
 
-    lax.fori_loop(0, 4, restrict, 0)
+    lax.fori_loop(0, 4, restrict, 0, unroll=2)
     b1_group = Group()
     b1_group.start(blocks(B1, B1, both))
+    v_group = Group()
+    vx, vy, vc = ghosts(VQ, VP, 1, 1, 2)
+    v_group.start(vx + vy + vc)
 
     wait_c1()
     S2[gx] = jnp.sum(S1[...], axis=0)
@@ -447,7 +455,7 @@
                 C1[c, k, x] = value * inverse
         return carry
 
-    lax.fori_loop(2, 14, coefficients1, 0)
+    lax.fori_loop(2, 14, coefficients1, 0, unroll=2)
 
     def weighted1(A, c, x):
         o = 1 - c
@@ -464,7 +472,7 @@
             A[c, x, near1] = weighted1(A, c, x)
             return carry
 
-        lax.fori_loop(0, 16 - 2 * low, rows, 0)
+        lax.fori_loop(0, 16 - 2 * low, rows, 0, unroll=8 - low)
 
     b1_group.wait()
 
@@ -472,7 +480,7 @@
         V1[0, x, near1] = B1[0, x, near1] * I1[0, x]
         return carry
 
-    lax.fori_loop(2, 14, first1, 0)
+    lax.fori_loop(2, 14, first1, 0, unroll=4)
     half_sweep1(V1, 1, 3)
     half_sweep1(V1, 0, 4)
     half_sweep1(V1, 1, 5)
@@ -490,15 +498,11 @@
     for copy in table_copies:
         copy.wait()
     depth = pl.ds(0, LANES)
-    G1[gy] = dot(Z[...], STK[depth, :])
+    G1[gy] = dot(Z[pl.ds(0, 8), :], STK[depth, :])
     finish = gather(G1, False)
     one = pl.ds(1, 1)
     v1_group = Group()
     v1_group.start(blocks(V1, VB, one) + second(V1, VB, one, ((2, 9, 1), (-2, 6, 14))))
-    v_group = Group()
-    vx, vy, vc = ghosts(VQ, VP, 1, 1, 2)
-    v_group.start(vy)
-
     wait_c2()
     CR[...] = jnp.sum(S2[...], axis=0)
     mean = [jnp.sum(jnp.where(lane == d, CR[...], 0.0), axis=1, keepdims=True) for d in range(3)]
@@ -510,13 +514,12 @@
         DI[tile, :] = 1.0 / ((flat_part + mean[0] * STK[pl.ds(pl.multiple_of(LANES + 8 * i, 8), 8), :]) * cells)
         return carry
 
-    lax.fori_loop(0, gxn, eigen, 0)
+    lax.fori_loop(0, gxn, eigen, 0, unroll=4)
     VB[1, pl.ds(6, 4), mine] = V1[1, pl.ds(6, 4), mine]
     VP[1, pl.ds(4, LX), own] = VQ[1, pl.ds(4, LX), own]
     finish()
     G2[gx] = dot(FI[...], G1[...].reshape(8 * gyn, LANES))
     finish = gather(G2, True)
-    v_group.start(vx + vc)
     column_x = (iota((16, 32 * gyn), 1) >> 2) & 7
     for x in range(8):
         M3[pl.ds(16 * x, 16), :] = jnp.where(column_x == x, LT[...], 0.0)
@@ -548,10 +551,10 @@
             T[i, pl.ds(h, 12, stride=4), :] = part
             T[i, pl.ds(h + 2, 12, stride=4), :] = part
         for x in (2 * i, 2 * i + 1):
-            VP[1, x, wide] = VP[1, x, wide] + T[i]
-        return carry
-
-    lax.fori_loop(1, 7, prolong, 0)
+            VP[1, x, wide] = VP[1, x, wide] + T[i, pl.ds(0, 48)]
+        return carry
+
+    lax.fori_loop(1, 7, prolong, 0, unroll=3)
     half_sweep(VP, 0, VP, True)
     exchanged(VP, 1, V)
     half_sweep(V, 0, V, True)
@@ -588,7 +591,7 @@
                 V((2, 6, 16, 48, LANES), F32),
                 V((2, 16, 48, LANES), F32),
                 V((2, 16, 48, LANES), F32),
-                V((8, 48, LANES), F32),
+                V((8, 64, LANES), F32),
                 V((6, 16, 40, LANES), F32),
                 V((2, 16, 24, LANES), F32),
                 V((2, 16, 24, LANES), F32),
@@ -596,8 +599,8 @@
                 V((2, 16, 40, LANES), F32),
                 V((2, 16, 40, LANES), F32),
                 V((2, 16, 40, LANES), F32),
-                V((40, LANES), F32),
-                V((8, LANES), F32),
+                V((48, LANES), F32),
+                V((16, LANES), F32),
                 V((gyn, 8, LANES), F32),
                 V((gxn, 8, LANES), F32),
                 V((gyn, 32, LANES), F32),

time: 79 us -> 69.6 us (0.88)
  Pallas kernels: 77.2 us -> 67.8 us
    pallas_call x1, Pallas kernels: 77.2 us -> 67.8 us  [step(): pl.pallas_call(functools.partial(kernel, gxn, gyn), out_shape=jax.ShapeDt...]
where the time goes in v4:
time: 69.6 us; the launch traced here: 69.4 us
  Pallas kernels  67.8 us (97%)
  local copies, waits for them, and re-layouts  1.67 us (2%)
    pallas_call x1, Pallas kernels, step(): pl.pallas_call(functools.partial(kernel, gxn, gyn), out_shape=jax.ShapeDt...  67.8 us
    unnamed x1, local copies, waits for them, and re-layouts  1.67 us

profile of v4, /device:TPU:1, one launch (start us, length us, event | category | flops | bytes accessed | tf_op | source)
XLA Modules:
  0.0 69.4 jit_solution(11018003417393883680)
XLA Ops:
  0.0 67.8 %cycle.1 = f32[8,16,512]{2,1,0:T(8,128)} custom-call(f32[8,16,512]{2,1,0:T(8,128)} %src_ref.1, bf16[3,8,16,512]{3,2,1,0:T(8,128)(2,1)} %coef_ref.1, f32[392,128]{1,0:T(8,128)} %constant.12.clone.stacked_hbm, f32[536,256]{1,0:T(8,128)} %constant.13.clone.alongx_hbm, f32[16,8,128]{2,1,0:T(8,128)} %constant.14.clone.first_hbm, ...), custom_call_target="tpu_custom_call" | custom-call | tf_op jit(solution)/shard_map/cycle/pallas_call | solution.py:581
  67.8 1.7 %copy.10 = f32[8,16,512]{2,1,0:T(8,128)} copy(f32[8,16,512]{2,1,0:T(8,128)} %cycle.1) | data formatting | bytes 524288
